TPU v7x, 32 devices: a whole 2x2x4 slice. The times are simulated.
32 devices in a mesh: gx: 4 (over z), gy: 8 (over y, x, core).
Axes of the slice: x: 2, y: 2, z: 4, core: 2. Of those that a mesh axis runs over, the one named last changes fastest.
Arguments:
- reference_scan: bfloat16 [128, 256, 128], P('gx', 'gy'), may hold values from -6 to 6
- deformed_scan: bfloat16 [128, 256, 128], P('gx', 'gy'), may hold values from -6 to 6
- source_column: int32 [4, 8, 64, 1], P('gx'), may hold values from 0 to 7, as said below
Outputs:
- update: float32 [3, 8, 16, 9], P(None, 'gx', 'gy')
- cg_residual: float32 [3, 8, 16, 9], P(None, 'gx', 'gy')
Inputs may be any that keep to these rules, and one draw needn't show every extreme that they name: source_column[p, q, b, 0] is q - 1, q or q + 1. Within one brick's 64 blocks at most 16 come from column q - 1 and at most 16 from column q + 1; in every draw some brick takes exactly 16 blocks from column q - 1 and some brick exactly 16 from column q + 1.
All inputs are finite; a program needn't handle non-finite values.
Results may differ from a plain program's by a relative error of at most 0.0003.
Values may be sent and summed in bfloat16 or wider, within the bound.
No kernel may reach another device: no remote copies, remote signals or barrier semaphores. Data moves between devices by JAX's collectives and lax.ppermute only.
A program may use at most 64 MiB of HBM per device.

v0:
```python
import jax
import jax.numpy as jnp
from jax import lax
from jax.sharding import PartitionSpec as P

E = 16
ITERS = 4


damping = 0.1


def extended(cells, sides, width):
    for axis, dim in sides:
        count = lax.axis_size(axis)
        ends = count - 1
        head = lax.slice_in_dim(cells, 0, width, axis=dim)
        tail = lax.slice_in_dim(cells, cells.shape[dim] - width, cells.shape[dim], axis=dim)
        cells = jnp.concatenate(
            [
                lax.ppermute(tail, axis, [(i, (i + 1) % count) for i in range(ends)]),
                cells,
                lax.ppermute(head, axis, [((i + 1) % count, i) for i in range(ends)]),
            ],
            axis=dim,
        )
    return cells


def passed_along(value, axis, steps):
    count = lax.axis_size(axis)
    leading, last = (max(0, -steps), min(count, count - steps))
    return lax.ppermute(value, axis, [(source, source + steps) for source in range(leading, last)])


def shape_matrix(count, nodes, edge):
    position = jnp.arange(count, dtype=jnp.float32)[:, None]
    anchor = jnp.arange(nodes, dtype=jnp.float32)[None, :] * edge
    return jnp.maximum(0.0, 1.0 - jnp.abs(position - anchor) / edge)


def to_blocks(brick):
    first, second, third = brick.shape
    pieces = brick.reshape(first // 8, 8, second // 8, 8, 4, third // 4)
    return pieces.transpose(0, 2, 4, 1, 3, 5).reshape(-1, 16 * third)


def from_blocks(blocks, first, second, third):
    pieces = blocks.reshape(first // 8, second // 8, 4, 8, 8, third // 4)
    return pieces.transpose(0, 3, 1, 4, 2, 5).reshape(first, second, third)


def inner(left, right):
    return jnp.sum(left * right)


def local(reference_scan, deformed_scan, source_column):
    cells_first, cells_second, cells_third = reference_scan.shape
    own_blocks = to_blocks(deformed_scan)
    table = source_column[0, :, :, 0]
    column = lax.axis_index("gy")
    wanted = lax.dynamic_index_in_dim(table, column, 0, keepdims=False)
    widened = extended(deformed_scan, (("gy", 1),), cells_second)
    lower_blocks = to_blocks(widened[:, :cells_second])
    upper_blocks = to_blocks(widened[:, 2 * cells_second :])
    offset = (wanted - column)[:, None]
    fetched = jnp.where(
        offset < 0, lower_blocks, jnp.where(offset > 0, upper_blocks, own_blocks)
    ).astype(jnp.float32)
    warped = from_blocks(fetched, cells_first, cells_second, cells_third)
    rimmed = extended(reference_scan, (("gx", 0), ("gy", 1)), 1)
    padded = jnp.pad(rimmed.astype(jnp.float32), ((0, 0), (0, 0), (1, 1)))
    scale = 1.0 / (2.0 * E)
    gradient = jnp.stack(
        [
            (padded[2:, 1:-1, 1:-1] - padded[:-2, 1:-1, 1:-1]) * scale,
            (padded[1:-1, 2:, 1:-1] - padded[1:-1, :-2, 1:-1]) * scale,
            (padded[1:-1, 1:-1, 2:] - padded[1:-1, 1:-1, :-2]) * scale,
        ]
    )
    misfit = padded[1:-1, 1:-1, 1:-1] - warped
    nodes_first = cells_first // E
    nodes_second = cells_second // E
    nodes_third = cells_third // E + 1
    matrix_x = shape_matrix(cells_first, nodes_first + 1, float(E))
    matrix_y = shape_matrix(cells_second, nodes_second + 1, float(E))
    matrix_z = shape_matrix(cells_third, nodes_third, float(E))
    highest = lax.Precision.HIGHEST

    def extend(nodal):
        upper_x = passed_along(nodal[:, 0], "gx", -1)
        wider = jnp.concatenate([nodal, upper_x[:, None]], axis=1)
        upper_y = passed_along(wider[:, :, 0], "gy", -1)
        return jnp.concatenate([wider, upper_y[:, :, None]], axis=2)

    def spread(nodal):
        temp = jnp.einsum("cijk,zk->cijz", nodal, matrix_z, precision=highest)
        temp = jnp.einsum("cijz,yj->ciyz", temp, matrix_y, precision=highest)
        return jnp.einsum("ciyz,xi->cxyz", temp, matrix_x, precision=highest)

    def fold_back(voxels):
        temp = jnp.einsum("cxyz,xi->ciyz", voxels, matrix_x, precision=highest)
        temp = jnp.einsum("ciyz,yj->cijz", temp, matrix_y, precision=highest)
        nodal = jnp.einsum("cijz,zk->cijk", temp, matrix_z, precision=highest)
        lower_y = passed_along(nodal[:, :, -1], "gy", 1)
        nodal = nodal[:, :, :-1].at[:, :, 0].add(lower_y)
        lower_x = passed_along(nodal[:, -1], "gx", 1)
        return nodal[:, :-1].at[:, 0].add(lower_x)

    def operate(nodal):
        moved = spread(extend(nodal))
        along = jnp.sum(gradient * moved, axis=0)
        return fold_back(gradient * along[None]) + damping * nodal

    rhs = fold_back(gradient * misfit[None])
    update = jnp.zeros_like(rhs)
    residual = rhs

    def paired(vector, image):
        return lax.psum((inner(vector, vector), inner(vector, image)), ("gx", "gy"))

    image = operate(residual)
    norm_now, product = paired(residual, image)
    alpha = norm_now / product
    direction = residual
    carried = image
    for turn in range(ITERS):
        update = update + alpha * direction
        residual = residual - alpha * carried
        if turn + 1 < ITERS:
            image = operate(residual)
            norm_next, product = paired(residual, image)
            ratio = norm_next / norm_now
            alpha = norm_next / (product - ratio * norm_next / alpha)
            direction = residual + ratio * direction
            carried = image + ratio * carried
            norm_now = norm_next
    return (update, residual)


def solution(mesh):
    return jax.shard_map(
        local,
        mesh=mesh,
        in_specs=(P("gx", "gy", None), P("gx", "gy", None), P("gx", None, None, None)),
        out_specs=(P(None, "gx", "gy", None), P(None, "gx", "gy", None)),
        check_vma=False,
    )
```

profile of v0, /device:TPU:0, one launch (start us, length us, event | category | flops | bytes accessed | tf_op | source)
XLA Modules:
  0.0 318.9 jit_solution(9763803837727632394)
XLA Ops:
  0.6 2.4 collective-permute-start.4
  6.4 4.9 %collective-permute-start = (bf16[1,32,128]{2,1,0:T(8,128)(2,1)S(1)}, bf16[1,32,128]{2,1,0:T(8,128)(2,1)S(1)}, u32[]{:S(2)}, u32[]{:S(2)}) collective-permute-start(bf16[1,32,128]{2,1,0:T(8,128)(2,1)S(1)} %get-tuple-element.149), channel_id=1, source_target_pairs={{0,8},{8,16},{16,24},{1,9},{9,17},{17,25},{2,10},{10,18},{18,26},{... | collective-permute-start | bytes 24584 | tf_op jit(solution)/shard_map/ppermute | solution.py:21
  13.7 3.6 %collective-permute-start.2 = (bf16[34,1,128]{2,1,0:T(2,128)(2,1)S(1)}, bf16[34,1,128]{2,1,0:T(2,128)(2,1)S(1)}, u32[]{:S(2)}, u32[]{:S(2)}) collective-permute-start(bf16[34,1,128]{2,1,0:T(2,128)(2,1)S(1)} %get-tuple-element.146), channel_id=1, source_target_pairs={{0,1},{1,2},{2,3},{3,4},{4,5},{5,6},{6,7},{8,9},{9,10},{10,11},{11... | collective-permute-start | bytes 26120 | tf_op jit(solution)/shard_map/ppermute | solution.py:21
  23.8 1.7 fusion.12
  26.1 4.4 %collective-permute-start.6 = (f32[3,3,9]{2,1,0:T(4,128)S(1)}, f32[3,3,9]{2,1,0:T(4,128)S(1)}, u32[]{:S(2)}, u32[]{:S(2)}) collective-permute-start(f32[3,3,9]{2,1,0:T(4,128)S(1)} %bitcast.232), channel_id=1, source_target_pairs={{0,1},{1,2},{2,3},{3,4},{4,5},{5,6},{6,7},{8,9},{9,10},{10,11},{11... | collective-permute-start | bytes 980 | tf_op jit(solution)/shard_map/ppermute | solution.py:33
  31.3 4.2 %collective-permute-start.7 = (f32[3,2,9]{2,1,0:T(2,128)S(1)}, f32[3,2,9]{2,1,0:T(2,128)S(1)}, u32[]{:S(2)}, u32[]{:S(2)}) collective-permute-start(f32[3,2,9]{2,1,0:T(2,128)S(1)} %slice_bitcast_fusion.7), channel_id=1, source_target_pairs={{0,8},{8,16},{16,24},{1,9},{9,17},{17,25},{2,10},{10,18},{18,26},{... | collective-permute-start | bytes 656 | tf_op jit(solution)/shard_map/ppermute | solution.py:33
  38.1 4.5 %collective-permute-done.8 = f32[3,2,9]{2,1,0:T(2,128)S(1)} collective-permute-done((f32[3,2,9]{2,1,0:T(2,128)S(1)}, f32[3,2,9]{2,1,0:T(2,128)S(1)}, u32[]{:S(2)}, u32[]{:S(2)}) %collective-permute-start.8) | collective-permute-done | bytes 248 | tf_op jit(solution)/shard_map/ppermute | solution.py:33
  43.9 1.8 collective-permute-done.9
  51.2 6.0 %collective-permute-start.10 = (f32[3,3,9]{2,1,0:T(4,128)S(1)}, f32[3,3,9]{2,1,0:T(4,128)S(1)}, u32[]{:S(2)}, u32[]{:S(2)}) collective-permute-start(f32[3,3,9]{2,1,0:T(4,128)S(1)} %bitcast.233), channel_id=1, source_target_pairs={{0,1},{1,2},{2,3},{3,4},{4,5},{5,6},{6,7},{8,9},{9,10},{10,11},{11... | collective-permute-start | bytes 980 | tf_op jit(solution)/shard_map/ppermute | solution.py:33
  58.1 3.9 %collective-permute-start.11 = (f32[3,2,9]{2,1,0:T(2,128)S(1)}, f32[3,2,9]{2,1,0:T(2,128)S(1)}, u32[]{:S(2)}, u32[]{:S(2)}) collective-permute-start(f32[3,2,9]{2,1,0:T(2,128)S(1)} %slice_bitcast_fusion.6), channel_id=1, source_target_pairs={{0,8},{8,16},{16,24},{1,9},{9,17},{17,25},{2,10},{10,18},{18,26},{... | collective-permute-start | bytes 656 | tf_op jit(solution)/shard_map/ppermute | solution.py:33
  63.9 44.2 %all-reduce.4 = (f32[]{:T(128)}, f32[]{:T(128)}) all-reduce(f32[]{:T(128)} %get-tuple-element.129, f32[]{:T(128)} %get-tuple-element.128), channel_id=1, replica_groups=mesh['gx'=4,'gy'=8] {'gx','gy'}, use_global_device_ids=true, to_apply=%region_1.2 | all-reduce | flops 2 | bytes 16 | tf_op jit(solution)/shard_map/psum | solution.py:120
  110.8 4.2 %collective-permute-done.12 = f32[3,2,9]{2,1,0:T(2,128)S(1)} collective-permute-done((f32[3,2,9]{2,1,0:T(2,128)S(1)}, f32[3,2,9]{2,1,0:T(2,128)S(1)}, u32[]{:S(2)}, u32[]{:S(2)}) %collective-permute-start.12) | collective-permute-done | bytes 248 | tf_op jit(solution)/shard_map/ppermute | solution.py:33
  123.7 4.4 %collective-permute-start.14 = (f32[3,3,9]{2,1,0:T(4,128)S(1)}, f32[3,3,9]{2,1,0:T(4,128)S(1)}, u32[]{:S(2)}, u32[]{:S(2)}) collective-permute-start(f32[3,3,9]{2,1,0:T(4,128)S(1)} %bitcast.234), channel_id=1, source_target_pairs={{0,1},{1,2},{2,3},{3,4},{4,5},{5,6},{6,7},{8,9},{9,10},{10,11},{11... | collective-permute-start | bytes 980 | tf_op jit(solution)/shard_map/ppermute | solution.py:33
  129.0 1.9 collective-permute-start.15
  132.9 42.5 %all-reduce.3 = (f32[]{:T(128)}, f32[]{:T(128)}) all-reduce(f32[]{:T(128)} %get-tuple-element.127, f32[]{:T(128)} %get-tuple-element.126), channel_id=1, replica_groups=mesh['gx'=4,'gy'=8] {'gx','gy'}, use_global_device_ids=true, to_apply=%region_6.7 | all-reduce | flops 2 | bytes 16 | tf_op jit(solution)/shard_map/psum | solution.py:120
  181.3 4.2 %collective-permute-done.16 = f32[3,2,9]{2,1,0:T(2,128)S(1)} collective-permute-done((f32[3,2,9]{2,1,0:T(2,128)S(1)}, f32[3,2,9]{2,1,0:T(2,128)S(1)}, u32[]{:S(2)}, u32[]{:S(2)}) %collective-permute-start.16) | collective-permute-done | bytes 248 | tf_op jit(solution)/shard_map/ppermute | solution.py:33
  186.8 1.8 collective-permute-done.17
  194.1 4.4 %collective-permute-start.18 = (f32[3,3,9]{2,1,0:T(4,128)S(1)}, f32[3,3,9]{2,1,0:T(4,128)S(1)}, u32[]{:S(2)}, u32[]{:S(2)}) collective-permute-start(f32[3,3,9]{2,1,0:T(4,128)S(1)} %bitcast.235), channel_id=1, source_target_pairs={{0,1},{1,2},{2,3},{3,4},{4,5},{5,6},{6,7},{8,9},{9,10},{10,11},{11... | collective-permute-start | bytes 980 | tf_op jit(solution)/shard_map/ppermute | solution.py:33
  199.4 1.9 collective-permute-start.19
  203.3 41.6 %all-reduce.2 = (f32[]{:T(128)}, f32[]{:T(128)}) all-reduce(f32[]{:T(128)} %get-tuple-element.125, f32[]{:T(128)} %get-tuple-element.124), channel_id=1, replica_groups=mesh['gx'=4,'gy'=8] {'gx','gy'}, use_global_device_ids=true, to_apply=%region_11.12 | all-reduce | flops 2 | bytes 16 | tf_op jit(solution)/shard_map/psum | solution.py:120
  250.1 4.2 %collective-permute-done.20 = f32[3,2,9]{2,1,0:T(2,128)S(1)} collective-permute-done((f32[3,2,9]{2,1,0:T(2,128)S(1)}, f32[3,2,9]{2,1,0:T(2,128)S(1)}, u32[]{:S(2)}, u32[]{:S(2)}) %collective-permute-start.20) | collective-permute-done | bytes 248 | tf_op jit(solution)/shard_map/ppermute | solution.py:33
  262.9 4.4 %collective-permute-start.22 = (f32[3,3,9]{2,1,0:T(4,128)S(1)}, f32[3,3,9]{2,1,0:T(4,128)S(1)}, u32[]{:S(2)}, u32[]{:S(2)}) collective-permute-start(f32[3,3,9]{2,1,0:T(4,128)S(1)} %bitcast.236), channel_id=1, source_target_pairs={{0,1},{1,2},{2,3},{3,4},{4,5},{5,6},{6,7},{8,9},{9,10},{10,11},{11... | collective-permute-start | bytes 980 | tf_op jit(solution)/shard_map/ppermute | solution.py:33
  268.2 1.9 collective-permute-start.23
  272.1 42.5 %all-reduce.1 = (f32[]{:T(128)}, f32[]{:T(128)}) all-reduce(f32[]{:T(128)} %get-tuple-element.123, f32[]{:T(128)} %get-tuple-element.122), channel_id=1, replica_groups=mesh['gx'=4,'gy'=8] {'gx','gy'}, use_global_device_ids=true, to_apply=%region_16.17 | all-reduce | flops 2 | bytes 16 | tf_op jit(solution)/shard_map/psum | solution.py:120
  (145 shorter events, 62.4 us)
Async XLA Ops:
  0.6 22.3 %collective-permute-start.4 = (bf16[32,32,128]{2,1,0:T(8,128)(2,1)}, bf16[32,32,128]{2,1,0:T(8,128)(2,1)S(1)}, u32[]{:S(2)}, u32[]{:S(2)}) collective-permute-start(bf16[32,32,128]{2,1,0:T(8,128)(2,1)} %param.24), channel_id=1, source_target_pairs={{0,1},{1,2},{2,3},{3,4},{4,5},{5,6},{6,7},{8,9},{9,10},{10,11},{11... | collective-permute-start | bytes 786440 | tf_op jit(solution)/shard_map/ppermute | solution.py:21
  3.1 19.9 %collective-permute-start.5 = (bf16[32,32,128]{2,1,0:T(8,128)(2,1)}, bf16[32,32,128]{2,1,0:T(8,128)(2,1)S(1)}, u32[]{:S(2)}, u32[]{:S(2)}) collective-permute-start(bf16[32,32,128]{2,1,0:T(8,128)(2,1)} %param.24), channel_id=1, source_target_pairs={{1,0},{2,1},{3,2},{4,3},{5,4},{6,5},{7,6},{9,8},{10,9},{11,10},{12... | collective-permute-start | bytes 786440 | tf_op jit(solution)/shard_map/ppermute | solution.py:23
  5.1 8.6 %collective-permute-start.1 = (bf16[1,32,128]{2,1,0:T(8,128)(2,1)S(1)}, bf16[1,32,128]{2,1,0:T(8,128)(2,1)S(1)}, u32[]{:S(2)}, u32[]{:S(2)}) collective-permute-start(bf16[1,32,128]{2,1,0:T(8,128)(2,1)S(1)} %get-tuple-element.148), channel_id=1, source_target_pairs={{8,0},{16,8},{24,16},{9,1},{17,9},{25,17},{10,2},{18,10},{26,18},{... | collective-permute-start | bytes 24584 | tf_op jit(solution)/shard_map/ppermute | solution.py:23
  6.4 6.3 %collective-permute-start = (bf16[1,32,128]{2,1,0:T(8,128)(2,1)S(1)}, bf16[1,32,128]{2,1,0:T(8,128)(2,1)S(1)}, u32[]{:S(2)}, u32[]{:S(2)}) collective-permute-start(bf16[1,32,128]{2,1,0:T(8,128)(2,1)S(1)} %get-tuple-element.149), channel_id=1, source_target_pairs={{0,8},{8,16},{16,24},{1,9},{9,17},{17,25},{2,10},{10,18},{18,26},{... | collective-permute-start | bytes 24584 | tf_op jit(solution)/shard_map/ppermute | solution.py:21
  13.7 8.0 %collective-permute-start.2 = (bf16[34,1,128]{2,1,0:T(2,128)(2,1)S(1)}, bf16[34,1,128]{2,1,0:T(2,128)(2,1)S(1)}, u32[]{:S(2)}, u32[]{:S(2)}) collective-permute-start(bf16[34,1,128]{2,1,0:T(2,128)(2,1)S(1)} %get-tuple-element.146), channel_id=1, source_target_pairs={{0,1},{1,2},{2,3},{3,4},{4,5},{5,6},{6,7},{8,9},{9,10},{10,11},{11... | collective-permute-start | bytes 26120 | tf_op jit(solution)/shard_map/ppermute | solution.py:21
  17.3 5.5 %collective-permute-start.3 = (bf16[34,1,128]{2,1,0:T(2,128)(2,1)S(1)}, bf16[34,1,128]{2,1,0:T(2,128)(2,1)S(1)}, u32[]{:S(2)}, u32[]{:S(2)}) collective-permute-start(bf16[34,1,128]{2,1,0:T(2,128)(2,1)S(1)} %get-tuple-element.147), channel_id=1, source_target_pairs={{1,0},{2,1},{3,2},{4,3},{5,4},{6,5},{7,6},{9,8},{10,9},{11,10},{12... | collective-permute-start | bytes 26120 | tf_op jit(solution)/shard_map/ppermute | solution.py:23
  26.1 5.2 %collective-permute-start.6 = (f32[3,3,9]{2,1,0:T(4,128)S(1)}, f32[3,3,9]{2,1,0:T(4,128)S(1)}, u32[]{:S(2)}, u32[]{:S(2)}) collective-permute-start(f32[3,3,9]{2,1,0:T(4,128)S(1)} %bitcast.232), channel_id=1, source_target_pairs={{0,1},{1,2},{2,3},{3,4},{4,5},{5,6},{6,7},{8,9},{9,10},{10,11},{11... | collective-permute-start | bytes 980 | tf_op jit(solution)/shard_map/ppermute | solution.py:33
  31.3 5.5 %collective-permute-start.7 = (f32[3,2,9]{2,1,0:T(2,128)S(1)}, f32[3,2,9]{2,1,0:T(2,128)S(1)}, u32[]{:S(2)}, u32[]{:S(2)}) collective-permute-start(f32[3,2,9]{2,1,0:T(2,128)S(1)} %slice_bitcast_fusion.7), channel_id=1, source_target_pairs={{0,8},{8,16},{16,24},{1,9},{9,17},{17,25},{2,10},{10,18},{18,26},{... | collective-permute-start | bytes 656 | tf_op jit(solution)/shard_map/ppermute | solution.py:33
  36.8 5.7 %collective-permute-start.8 = (f32[3,2,9]{2,1,0:T(2,128)S(1)}, f32[3,2,9]{2,1,0:T(2,128)S(1)}, u32[]{:S(2)}, u32[]{:S(2)}) collective-permute-start(f32[3,2,9]{2,1,0:T(2,128)S(1)} %get-tuple-element.152), channel_id=1, source_target_pairs={{8,0},{16,8},{24,16},{9,1},{17,9},{25,17},{10,2},{18,10},{26,18},{... | collective-permute-start | bytes 656 | tf_op jit(solution)/shard_map/ppermute | solution.py:33
  42.6 3.1 collective-permute-start.9
  51.2 6.8 %collective-permute-start.10 = (f32[3,3,9]{2,1,0:T(4,128)S(1)}, f32[3,3,9]{2,1,0:T(4,128)S(1)}, u32[]{:S(2)}, u32[]{:S(2)}) collective-permute-start(f32[3,3,9]{2,1,0:T(4,128)S(1)} %bitcast.233), channel_id=1, source_target_pairs={{0,1},{1,2},{2,3},{3,4},{4,5},{5,6},{6,7},{8,9},{9,10},{10,11},{11... | collective-permute-start | bytes 980 | tf_op jit(solution)/shard_map/ppermute | solution.py:33
  58.1 5.2 %collective-permute-start.11 = (f32[3,2,9]{2,1,0:T(2,128)S(1)}, f32[3,2,9]{2,1,0:T(2,128)S(1)}, u32[]{:S(2)}, u32[]{:S(2)}) collective-permute-start(f32[3,2,9]{2,1,0:T(2,128)S(1)} %slice_bitcast_fusion.6), channel_id=1, source_target_pairs={{0,8},{8,16},{16,24},{1,9},{9,17},{17,25},{2,10},{10,18},{18,26},{... | collective-permute-start | bytes 656 | tf_op jit(solution)/shard_map/ppermute | solution.py:33
  109.5 5.5 %collective-permute-start.12 = (f32[3,2,9]{2,1,0:T(2,128)S(1)}, f32[3,2,9]{2,1,0:T(2,128)S(1)}, u32[]{:S(2)}, u32[]{:S(2)}) collective-permute-start(f32[3,2,9]{2,1,0:T(2,128)S(1)} %slice_bitcast_fusion.5), channel_id=1, source_target_pairs={{8,0},{16,8},{24,16},{9,1},{17,9},{25,17},{10,2},{18,10},{26,18},{... | collective-permute-start | bytes 656 | tf_op jit(solution)/shard_map/ppermute | solution.py:33
  115.0 3.1 collective-permute-start.13
  123.7 5.3 %collective-permute-start.14 = (f32[3,3,9]{2,1,0:T(4,128)S(1)}, f32[3,3,9]{2,1,0:T(4,128)S(1)}, u32[]{:S(2)}, u32[]{:S(2)}) collective-permute-start(f32[3,3,9]{2,1,0:T(4,128)S(1)} %bitcast.234), channel_id=1, source_target_pairs={{0,1},{1,2},{2,3},{3,4},{4,5},{5,6},{6,7},{8,9},{9,10},{10,11},{11... | collective-permute-start | bytes 980 | tf_op jit(solution)/shard_map/ppermute | solution.py:33
  129.0 3.2 collective-permute-start.15
  180.0 5.5 %collective-permute-start.16 = (f32[3,2,9]{2,1,0:T(2,128)S(1)}, f32[3,2,9]{2,1,0:T(2,128)S(1)}, u32[]{:S(2)}, u32[]{:S(2)}) collective-permute-start(f32[3,2,9]{2,1,0:T(2,128)S(1)} %slice_bitcast_fusion.3), channel_id=1, source_target_pairs={{8,0},{16,8},{24,16},{9,1},{17,9},{25,17},{10,2},{18,10},{26,18},{... | collective-permute-start | bytes 656 | tf_op jit(solution)/shard_map/ppermute | solution.py:33
  185.5 3.1 collective-permute-start.17
  194.1 5.3 %collective-permute-start.18 = (f32[3,3,9]{2,1,0:T(4,128)S(1)}, f32[3,3,9]{2,1,0:T(4,128)S(1)}, u32[]{:S(2)}, u32[]{:S(2)}) collective-permute-start(f32[3,3,9]{2,1,0:T(4,128)S(1)} %bitcast.235), channel_id=1, source_target_pairs={{0,1},{1,2},{2,3},{3,4},{4,5},{5,6},{6,7},{8,9},{9,10},{10,11},{11... | collective-permute-start | bytes 980 | tf_op jit(solution)/shard_map/ppermute | solution.py:33
  199.4 3.2 %collective-permute-start.19 = (f32[3,2,9]{2,1,0:T(2,128)S(1)}, f32[3,2,9]{2,1,0:T(2,128)S(1)}, u32[]{:S(2)}, u32[]{:S(2)}) collective-permute-start(f32[3,2,9]{2,1,0:T(2,128)S(1)} %slice_bitcast_fusion.2), channel_id=1, source_target_pairs={{0,8},{8,16},{16,24},{1,9},{9,17},{17,25},{2,10},{10,18},{18,26},{... | collective-permute-start | bytes 656 | tf_op jit(solution)/shard_map/ppermute | solution.py:33
  248.8 5.5 %collective-permute-start.20 = (f32[3,2,9]{2,1,0:T(2,128)S(1)}, f32[3,2,9]{2,1,0:T(2,128)S(1)}, u32[]{:S(2)}, u32[]{:S(2)}) collective-permute-start(f32[3,2,9]{2,1,0:T(2,128)S(1)} %slice_bitcast_fusion.1), channel_id=1, source_target_pairs={{8,0},{16,8},{24,16},{9,1},{17,9},{25,17},{10,2},{18,10},{26,18},{... | collective-permute-start | bytes 656 | tf_op jit(solution)/shard_map/ppermute | solution.py:33
  254.3 3.1 collective-permute-start.21
  262.9 5.3 %collective-permute-start.22 = (f32[3,3,9]{2,1,0:T(4,128)S(1)}, f32[3,3,9]{2,1,0:T(4,128)S(1)}, u32[]{:S(2)}, u32[]{:S(2)}) collective-permute-start(f32[3,3,9]{2,1,0:T(4,128)S(1)} %bitcast.236), channel_id=1, source_target_pairs={{0,1},{1,2},{2,3},{3,4},{4,5},{5,6},{6,7},{8,9},{9,10},{10,11},{11... | collective-permute-start | bytes 980 | tf_op jit(solution)/shard_map/ppermute | solution.py:33
  268.2 3.2 collective-permute-start.23
  (1 other events, 3.4 us)
where the time goes:
time: 321 us; the launch traced here: 319 us
  blocking collectives  171 us (53%)
  starting transfers between devices  63.1 us (20%)
  waiting for transfers between devices  36.5 us (11%)
  matrix products  18.5 us (6%)
  between operations  15 us (5%)
  other arithmetic  10.7 us (3%)
  local copies, waits for them, and re-layouts  4.5 us (1%)
    psum x4, blocking collectives, paired(): return lax.psum((inner(vector, vector), inner(vector, image)), ('gx', 'gy'))  171 us
    ppermute x18, starting transfers between devices, passed_along(): lax.ppermute(value, axis, [(source, source + steps) for source in range(l...  48.3 us
    ppermute x18, waiting for transfers between devices, passed_along(): lax.ppermute(value, axis, [(source, source + steps) for source in range(l...  34.1 us
    ppermute x3, starting transfers between devices, extended(): lax.ppermute(tail, axis, [(i, (i + 1) % count) for i in range(ends)])  10.9 us
    dot_general x5, matrix products, fold_back(): temp = jnp.einsum('cxyz,xi->ciyz', voxels, matrix_x, precision=highest)  8.5 us
  transfers between devices with their start and end apart: 24, of which 20 were waited for; matrix products, arithmetic and copies ran while one was open for 2% of the time, Pallas kernels for 0%

commit v1 on v0

v1 whole, which is shorter than its diff:
```python
import functools

import jax
import jax.numpy as jnp
import numpy as np
from jax import lax
from jax.experimental import pallas as pl
from jax.experimental.pallas import tpu as pltpu
from jax.sharding import PartitionSpec as P

E = 16
ITERS = 4
NZN = 9
OWN = 12 * NZN


damping = 0.1


def weights():
    m = np.arange(E, 0, -1, dtype=np.float64) / E
    same_low, cross, same_high, low, high = m * m, m * (1 - m), (1 - m) ** 2, m, 1 - m

    def along(count):
        d = np.zeros((count + 1, count * E))
        o = np.zeros((count + 1, count * E))
        h = np.zeros((count + 1, count * E))
        for e in range(count):
            at = slice(e * E, (e + 1) * E)
            d[e, at] += same_low
            d[e + 1, at] += same_high
            o[e, at] += cross
            h[e, at] += low
            h[e + 1, at] += high
        return d, o, h

    yd, yo, yh = along(2)
    w = np.zeros((48, 160))
    for s in range(2):
        for tx in range(2):
            k = slice((s * 2 + tx) * 32, (s * 2 + tx) * 32 + 32)
            for iy in range(2):
                w[iy * 8 + s * 4 + tx * 2 + 0, k] = yd[iy]
                w[iy * 8 + s * 4 + tx * 2 + 1, k] = yo[iy]
            w[16 + s * 2 + tx, k] = yd[2]
        k = slice(s * 64, s * 64 + 32)
        for iy in range(2):
            w[24 + iy * 4 + s * 2 + 0, k] = yd[iy]
            w[24 + iy * 4 + s * 2 + 1, k] = yo[iy]
        w[(32 if s == 0 else 40) + 7, k] = yd[2]
    for iy in range(3):
        w[20 + iy, 128:160] = yh[iy]
        w[32 + 4 + iy, 128:160] = yh[iy]
    zd, zo, zh = along(8)
    z = np.zeros((128, 128))
    scale = 1.0 / (2.0 * E)
    z[:, 0:9] = zd.T * scale * scale
    z[:, 9:18] = zo.T * scale * scale
    z[:, 18:27] = zh.T * scale
    return w.astype(np.float32), z.astype(np.float32)


def split3(value):
    high = value.astype(jnp.bfloat16)
    rest = value - high.astype(jnp.float32)
    mid = rest.astype(jnp.bfloat16)
    low = (rest - mid.astype(jnp.float32)).astype(jnp.bfloat16)
    return high, mid, low


def pack_kernel(f_ref, d_ref, ya_ref, yb_ref, xa_ref, xb_ref):
    even_x = lax.rem(lax.axis_index("gx"), 2) == 0
    even_y = lax.rem(lax.axis_index("gy"), 2) == 0
    bx, by, _ = f_ref.shape
    ya_ref[0:bx] = d_ref[...]
    yb_ref[0:bx] = d_ref[...]
    head, tail = f_ref[:, 0, :], f_ref[:, by - 1, :]
    ya_ref[bx] = jnp.where(even_y, tail, head)
    yb_ref[bx] = jnp.where(even_y, head, tail)
    xa_ref[...] = jnp.where(even_x, f_ref[bx - 1], f_ref[0])
    xb_ref[...] = jnp.where(even_x, f_ref[0], f_ref[bx - 1])


PAIRS = ((0, 0), (1, 1), (2, 2), (0, 1), (1, 2), (2, 0))


def assemble_kernel(f_ref, d_ref, ra_ref, rb_ref, xa_ref, xb_ref, col_ref, w_ref, z_ref, out_ref, field, slope, misfit, source, moment):
    px, qy = lax.axis_index("gx"), lax.axis_index("gy")
    even_x, even_y = lax.rem(px, 2) == 0, lax.rem(qy, 2) == 0
    bx, by, bz = f_ref.shape
    f32 = jnp.float32
    lane = lax.broadcasted_iota(jnp.int32, (8, bz), 1)
    sign = jnp.where(even_y, 1, -1)
    for i in range(bx // 8):
        for j in range(by // 8):
            code = jnp.zeros((8, bz), jnp.int32)
            for k in range(4):
                at = (col_ref[qy, (i * (by // 8) + j) * 4 + k] - qy) * sign
                code = jnp.where(lane // (bz // 4) == k, at, code)
            source[i, j * 8 : j * 8 + 8, :] = code
    field[0, 8 : 8 + by, :] = jnp.where(even_x, xb_ref[...], xa_ref[...]).astype(f32)
    field[bx + 1, 8 : 8 + by, :] = jnp.where(even_x, xa_ref[...], xb_ref[...]).astype(f32)
    rim_a, rim_b = ra_ref[bx].astype(f32), rb_ref[bx].astype(f32)
    field[1 : bx + 1, 7, :] = jnp.where(even_y, rim_b, rim_a)
    field[1 : bx + 1, 8 + by, :] = jnp.where(even_y, rim_a, rim_b)

    def prepare(x, _):
        here = f_ref[x].astype(f32)
        field[x + 1, 8 : 8 + by, :] = here
        slope[x] = field[x + 1, 9 : 9 + by, :] - field[x + 1, 7 : 7 + by, :]
        code = source[x // 8]
        warped = jnp.where(code == 0, d_ref[x].astype(f32), jnp.where(code > 0, ra_ref[x].astype(f32), rb_ref[x].astype(f32)))
        misfit[x] = here - warped
        return 0

    lax.fori_loop(0, bx, prepare, 0)

    def group(g, _):
        rows = pl.ds(pl.multiple_of(g * 8, 8), 8)
        rows_f = pl.ds(pl.multiple_of(g * 8 + 8, 8), 8)
        found = []
        for e in range(2):
            before, now = field[e * E, rows_f, :], field[e * E + 1, rows_f, :]
            tot = [[jnp.zeros((8, bz), f32) for _ in range(3)] for _ in range(6)]
            right = [[jnp.zeros((8, bz), f32) for _ in range(2)] for _ in range(3)]
            for t in range(E):
                x = e * E + t
                after = field[x + 2, rows_f, :]
                up = jnp.where(lane == bz - 1, 0.0, pltpu.roll(now, bz - 1, 1))
                down = jnp.where(lane == 0, 0.0, pltpu.roll(now, 1, 1))
                grad = (after - before, slope[x, rows, :], up - down)
                for n, (c, d) in enumerate(PAIRS):
                    tot[n][0] = tot[n][0] + grad[c] * grad[d]
                    tot[n][1] = tot[n][1] + tot[n][0]
                    tot[n][2] = tot[n][2] + tot[n][1]
                miss = misfit[x, rows, :]
                for c in range(3):
                    right[c][0] = right[c][0] + grad[c] * miss
                    right[c][1] = right[c][1] + right[c][0]
                before, now = now, after
            ent = []
            for n in range(6):
                a0, a1, a2 = tot[n]
                sq = 2.0 * a2 - a1
                ent.append((sq * (1 / 256), (16.0 * a1 - sq) * (1 / 256), a0 - a1 * (1 / 8) + sq * (1 / 256)))
            rh = [(right[c][1] * (1 / 16), right[c][0] - right[c][1] * (1 / 16)) for c in range(3)]
            found.append((ent, rh))
        for s in range(2):
            for c in range(3):
                e0, e1 = found[0][0][s * 3 + c], found[1][0][s * 3 + c]
                same = (e0[0], e0[2] + e1[0], e1[2])
                cross = (e0[1], e1[1], jnp.zeros((8, bz), f32))
                for ix in range(3):
                    at = slice((c * 3 + ix) * bz, (c * 3 + ix + 1) * bz)
                    moment[pl.ds(pl.multiple_of(s * 64 + g * 8, 8), 8), at] = same[ix]
                    moment[pl.ds(pl.multiple_of(s * 64 + 32 + g * 8, 8), 8), at] = cross[ix]
        for c in range(3):
            r0, r1 = found[0][1][c], found[1][1][c]
            for ix, value in enumerate((r0[0], r0[1] + r1[0], r1[1])):
                at = slice((c * 3 + ix) * bz, (c * 3 + ix + 1) * bz)
                moment[pl.ds(pl.multiple_of(128 + g * 8, 8), 8), at] = value
        return 0

    lax.fori_loop(0, by // 8, group, 0)

    w = w_ref[...]
    along_y = 0.0
    for part in split3(moment[...]):
        along_y = along_y + jnp.dot(w, part, preferred_element_type=f32)
    stacked = jnp.concatenate(
        [along_y[(24 if ix == 2 else 0) : (48 if ix == 2 else 24), (c * 3 + ix) * bz : (c * 3 + ix + 1) * bz] for c in range(3) for ix in range(3)],
        axis=0,
    )
    z = z_ref[...]
    along_z = 0.0
    for part in split3(stacked):
        along_z = along_z + jnp.dot(part, z, preferred_element_type=f32)

    slot = lane // NZN
    row = lax.broadcasted_iota(jnp.int32, (8, bz), 0)
    rows_out = [jnp.zeros((8, bz), f32) for _ in range(3)]

    def place(group_at, value, src, dst, mask=None):
        shift = ((dst - src) * NZN) % bz
        moved = pltpu.roll(value, shift, 1) if shift else value
        keep = slot == dst
        if mask is not None:
            keep = keep & mask
        rows_out[group_at] = jnp.where(keep, moved, rows_out[group_at])

    for c in range(3):
        for ix in range(2):
            at = (c * 3 + ix) * 24
            base = c * 4 + ix * 2
            v0, v1, v2 = (along_z[at + i * 8 : at + i * 8 + 8] for i in range(3))
            for tz in range(2):
                place(tz, v0, tz, base)
                place(tz, v1, tz, base + 1)
                place(2, v2, tz, base + tz, row < 4)
            place(2, v2, 2, base, (row >= 4) & (row < 7))
        at = (c * 3 + 2) * 24
        v0, v1, v2 = (along_z[at + i * 8 : at + i * 8 + 8] for i in range(3))
        for tz in range(2):
            place(c, v0, tz, 12 + tz, (row < 4) if c == 2 else None)
            place(2, v1, tz, c * 4 + tz, row == 7)
            place(2, v2, tz, c * 4 + 2 + tz, row == 7)
        place(2, v1, 2, c * 4 + 1, (row >= 4) & (row < 7))
        if c == 2:
            for tz in range(2):
                place(2, v0, tz, 12 + tz, row >= 4)
    for i in range(3):
        out_ref[i * 8 : i * 8 + 8, :] = rows_out[i]


def solve_kernel(gx, gy, mine_ref, other_ref, up_ref, res_ref, rows, table, vectors):
    count = gx * gy
    px, qy = lax.axis_index("gx"), lax.axis_index("gy")
    odd = lax.rem(qy, 2)
    f32 = jnp.float32
    for i in range(count // 2):
        rows[:, 2 * i + odd, :] = mine_ref[i]
        rows[:, 2 * i + 1 - odd, :] = other_ref[i]
    shape = (count, 128)
    lane = lax.broadcasted_iota(jnp.int32, shape, 1)
    device = lax.broadcasted_iota(jnp.int32, shape, 0)
    q = lax.rem(device, gy)
    slot = lane // NZN
    own = lane < OWN
    ix1 = lax.rem(slot, 4) >= 2
    iy1 = lax.rem(slot, 2) == 1
    corner = own & (lax.rem(slot, 4) == 0)
    x_low = own & ~ix1
    y_low = own & ~iy1
    first_p, last_p = device < gy, device >= count - gy
    first_q, last_q = q == 0, q == gy - 1

    def lanes(value, shift):
        shift = shift % 128
        return pltpu.roll(value, shift, 1) if shift else value

    def down(value, shift):
        shift = shift % count
        return pltpu.roll(value, shift, 0) if shift else value

    def from_below_x(value):
        return jnp.where(first_p, 0.0, down(value, gy))

    def from_below_y(value):
        return jnp.where(first_q, 0.0, down(value, 1))

    def slots(value, src, dst):
        return lanes(value, (dst - src) * NZN)

    def xp(v):
        return jnp.where(ix1, down(lanes(v, 18), -gy), lanes(v, -18))

    def xm(v):
        return jnp.where(ix1, lanes(v, 18), down(lanes(v, -18), gy))

    def yp(v):
        return jnp.where(iy1, down(lanes(v, 9), -1), lanes(v, -9))

    def ym(v):
        return jnp.where(iy1, lanes(v, 9), down(lanes(v, -9), 1))

    def turn(v, j):
        if j == 1:
            return jnp.where(lane < 72, lanes(v, -36), lanes(v, 72))
        return jnp.where(lane < 36, lanes(v, -72), lanes(v, 36))

    for s in range(2):
        for tx in range(2):
            for ty in range(2):
                for tz in range(2):
                    entry = jnp.where(own, rows[tz * 8 + s * 4 + tx * 2 + ty], 0.0)
                    if ty == 0:
                        spill = slots(rows[16 + s * 2 + tx], tz, 0)
                        entry = entry + from_below_y(jnp.where(y_low, spill, 0.0))
                    if tx == 0:
                        spill = jnp.zeros(shape, f32)
                        for c in range(3):
                            for iy in range(2):
                                moved = slots(rows[c * 8 + iy * 4 + s * 2 + ty], 12 + tz, c * 4 + iy)
                                spill = jnp.where(slot == c * 4 + iy, moved, spill)
                        if ty == 0:
                            both = slots(rows[23], s * 2 + tz, 0)
                            spill = spill + from_below_y(jnp.where(corner, both, 0.0))
                        entry = entry + from_below_x(spill)
                    if tx == 1:
                        entry = jnp.where(last_p & ix1, 0.0, entry)
                    if ty == 1:
                        entry = jnp.where(last_q & iy1, 0.0, entry)
                    for dx in (1, -1) if tx else (0,):
                        by_x = jnp.where(own, xm(entry), 0.0) if dx < 0 else entry
                        for dy in (1, -1) if ty else (0,):
                            by_y = jnp.where(own, ym(by_x), 0.0) if dy < 0 else by_x
                            for dz in (1, -1) if tz else (0,):
                                by_z = lanes(by_y, 1) if dz < 0 else by_y
                                offset = (dx + 1) * 9 + (dy + 1) * 3 + dz + 1
                                if s == 0:
                                    table[offset] = by_z
                                else:
                                    table[54 + offset] = by_z
                                    table[27 + offset] = turn(by_z, 2)

    r0, r1, r2 = rows[20], rows[21], rows[22]
    rhs = jnp.where(iy1, lanes(r1, 9), r0) + from_below_y(jnp.where(iy1, 0.0, r2))
    far = jnp.where(iy1, r1, lanes(r0, -9)) + from_below_y(jnp.where(iy1, 0.0, lanes(r2, -9)))
    rhs = rhs + from_below_x(jnp.where(ix1, 0.0, far))
    rhs = jnp.where(own, rhs, 0.0)

    def operate(v):
        parts = [jnp.zeros(shape, f32) for _ in range(3)]
        for dx in range(-1, 2):
            vx = v if dx == 0 else (xp(v) if dx > 0 else xm(v))
            for dy in range(-1, 2):
                vy = vx if dy == 0 else (yp(vx) if dy > 0 else ym(vx))
                for dz in range(-1, 2):
                    vz = lanes(vy, -dz)
                    offset = (dx + 1) * 9 + (dy + 1) * 3 + dz + 1
                    for s in range(3):
                        parts[s] = parts[s] + table[27 * s + offset] * vz
        coupled = parts[0] + turn(parts[1], 1) + turn(parts[2], 2)
        return damping * v + jnp.where(own, coupled, 0.0)

    def total(v):
        return jnp.sum(jnp.sum(v, axis=0, keepdims=True), axis=1, keepdims=True)

    update = jnp.zeros(shape, f32)
    residual = rhs
    direction = rhs
    norm_now = total(residual * residual)
    for turn_at in range(ITERS):
        image = operate(direction)
        alpha = norm_now / total(direction * image)
        update = update + alpha * direction
        residual = residual - alpha * image
        if turn_at + 1 < ITERS:
            norm_next = total(residual * residual)
            direction = residual + (norm_next / norm_now) * direction
            norm_now = norm_next
    vectors[0] = update
    vectors[1] = residual
    me = px * gy + qy
    for i, ref in enumerate((up_ref, res_ref)):
        line = vectors[i, pl.ds(me, 1), :]
        for c in range(3):
            for ix in range(2):
                for iy in range(2):
                    ref[c, ix, iy : iy + 1, :] = lanes(line, -(c * 4 + ix * 2 + iy) * NZN)[:, :NZN]


VMEM = pl.BlockSpec(memory_space=pltpu.VMEM)
SMEM = pl.BlockSpec(memory_space=pltpu.SMEM)


def matching(axis, start):
    count = lax.axis_size(axis)
    pairs = []
    for i in range(start, count - 1, 2):
        pairs += [(i, i + 1), (i + 1, i)]
    return pairs


def local(reference_scan, deformed_scan, source_column):
    bx, by, bz = reference_scan.shape
    gx, gy = lax.axis_size("gx"), lax.axis_size("gy")
    half = jnp.bfloat16
    ya, yb, xa, xb = pl.pallas_call(
        pack_kernel,
        out_shape=[jax.ShapeDtypeStruct((bx + 1, by, bz), half)] * 2 + [jax.ShapeDtypeStruct((by, bz), half)] * 2,
        in_specs=[VMEM] * 2,
        out_specs=[VMEM] * 4,
        name="pack",
    )(reference_scan, deformed_scan)
    rb = lax.ppermute(yb, "gy", matching("gy", 1))
    qa = lax.ppermute(xa, "gx", matching("gx", 0))
    qb = lax.ppermute(xb, "gx", matching("gx", 1))
    ra = lax.ppermute(ya, "gy", matching("gy", 0))
    w, z = weights()
    payload = pl.pallas_call(
        assemble_kernel,
        out_shape=jax.ShapeDtypeStruct((24, bz), jnp.float32),
        in_specs=[VMEM] * 6 + [SMEM] + [VMEM] * 2,
        out_specs=VMEM,
        scratch_shapes=[
            pltpu.VMEM((bx + 2, by + 16, bz), jnp.float32),
            pltpu.VMEM((bx, by, bz), jnp.float32),
            pltpu.VMEM((bx, by, bz), jnp.float32),
            pltpu.VMEM((bx // 8, by, bz), jnp.int32),
            pltpu.VMEM((160, 9 * bz), jnp.float32),
        ],
        name="assemble",
    )(reference_scan, deformed_scan, ra, rb, qa, qb, source_column[0, :, :, 0], jnp.asarray(w, half), jnp.asarray(z, half))
    groups = [[i * 2 + core for i in range(gx * gy // 2)] for core in range(2)]
    mine = lax.all_to_all(jnp.broadcast_to(payload[None], (gx * gy // 2, 24, bz)), ("gx", "gy"), 0, 0, axis_index_groups=groups)
    other = lax.ppermute(mine, "gy", [(i, i ^ 1) for i in range(gy)])
    out = jax.ShapeDtypeStruct((3, 2, 2, NZN), jnp.float32)
    update, residual = pl.pallas_call(
        functools.partial(solve_kernel, gx, gy),
        out_shape=[out, out],
        in_specs=[VMEM] * 2,
        out_specs=[VMEM] * 2,
        scratch_shapes=[
            pltpu.VMEM((24, gx * gy, bz), jnp.float32),
            pltpu.VMEM((81, gx * gy, bz), jnp.float32),
            pltpu.VMEM((2, gx * gy, bz), jnp.float32),
        ],
        name="solve",
    )(mine, other)
    return update, residual


def solution(mesh):
    return jax.shard_map(
        local,
        mesh=mesh,
        in_specs=(P("gx", "gy", None), P("gx", "gy", None), P("gx", None, None, None)),
        out_specs=(P(None, "gx", "gy", None), P(None, "gx", "gy", None)),
        check_vma=False,
    )
```

time: 321 us -> 42.5 us (0.13)
  blocking collectives: 171 us -> 21.9 us
  starting transfers between devices: 63.1 us -> 4.44 us
  waiting for transfers between devices: 36.5 us -> 2.63 us
  matrix products: 18.5 us -> 0 us
  between operations: 15 us -> 0.69 us
  other arithmetic: 10.7 us -> 0 us
  Pallas kernels: 0 us -> 10.4 us
    psum x4 -> x0, blocking collectives: 171 us -> none  [paired(): return lax.psum((inner(vector, vector), inner(vector, image)), ('gx', 'gy'))]
    ppermute x24 -> x5, starting transfers between devices: 63.1 us -> 4.44 us  [the longest x1 2.63 us: local(): qa = lax.ppermute(xa, 'gx', matching('gx', 0))]
    ppermute x24 -> x5, waiting for transfers between devices: 36.5 us -> 2.63 us  [the longest x1 1.44 us: local(): other = lax.ppermute(mine, 'gy', [(i, i ^ 1) for i in range(gy)])]
    all_to_all x0 -> x1, blocking collectives: none -> 21.9 us  [local(): lax.all_to_all(jnp.broadcast_to(payload[None], (gx * gy // 2, 24, bz)), (...]
    dot_general x27 -> x0, matrix products: 18.5 us -> none  [the longest x5 8.5 us: fold_back(): temp = jnp.einsum('cxyz,xi->ciyz', voxels, matrix_x, precision=highest)]
    pallas_call x0 -> x3, Pallas kernels: none -> 10.4 us  [the longest x1 4.68 us: local(): pl.pallas_call(functools.partial(solve_kernel, gx, gy), out_shape=[out, o...]
    reduce_sum x8 -> x0, other arithmetic: 7.25 us -> none  [the longest x4 4.64 us: operate(): along = jnp.sum(gradient * moved, axis=0)]
  transfers between devices with their start and end apart: 24 -> 5, of which waited for: 20 -> 2; matrix products, arithmetic and copies ran while one was open for 2% -> 0% of each run, Pallas kernels for 0% -> 0%
where the time goes in v1:
time: 42.5 us; the launch traced here: 42.2 us
  blocking collectives  21.9 us (52%)
  Pallas kernels  10.4 us (24%)
  starting transfers between devices  4.44 us (10%)
  waiting for transfers between devices  2.63 us (6%)
  local copies, waits for them, and re-layouts  2.17 us (5%)
  between operations  0.69 us (2%)
    all_to_all x1, blocking collectives, local(): lax.all_to_all(jnp.broadcast_to(payload[None], (gx * gy // 2, 24, bz)), (...  21.9 us
    pallas_call x1, Pallas kernels, local(): pl.pallas_call(functools.partial(solve_kernel, gx, gy), out_shape=[out, o...  4.68 us
    pallas_call x1, Pallas kernels, local(): pl.pallas_call(assemble_kernel, out_shape=jax.ShapeDtypeStruct((24, bz),...  3.82 us
    ppermute x1, starting transfers between devices, local(): qa = lax.ppermute(xa, 'gx', matching('gx', 0))  2.63 us
    pallas_call x1, Pallas kernels, local(): pl.pallas_call(pack_kernel, out_shape=[jax.ShapeDtypeStruct((bx + 1, by,...  1.92 us
    unnamed x12, local copies, waits for them, and re-layouts  1.45 us
    ppermute x1, waiting for transfers between devices, local(): other = lax.ppermute(mine, 'gy', [(i, i ^ 1) for i in range(gy)])  1.44 us
    ppermute x1, waiting for transfers between devices, local(): qa = lax.ppermute(xa, 'gx', matching('gx', 0))  1.18 us
  transfers between devices with their start and end apart: 5, of which 2 were waited for; matrix products, arithmetic and copies ran while one was open for 0% of the time, Pallas kernels for 0%

profile of v1, /device:TPU:0, one launch (start us, length us, event | category | flops | bytes accessed | tf_op | source)
XLA Modules:
  0.0 42.2 jit_solution(10203203574259133378)
XLA Ops:
  0.6 1.9 %pack.1 = (bf16[33,32,128]{2,1,0:T(8,128)(2,1)}, bf16[33,32,128]{2,1,0:T(8,128)(2,1)}, bf16[32,128]{1,0:T(8,128)(2,1)}, bf16[32,128]{1,0:T(8,128)(2,1)}) custom-call(bf16[32,32,128]{2,1,0:T(8,128)(2,1)} %f_ref.3, bf16[32,32,128]{2,1,0:T(8,128)(2,1)} %d_ref.3), custom_call_target="tpu_custom_call" | custom-call | tf_op jit(solution)/shard_map/pack/pallas_call | solution.py:369
  2.5 0.5 %collective-permute-start = (bf16[33,32,128]{2,1,0:T(8,128)(2,1)}, bf16[33,32,128]{2,1,0:T(8,128)(2,1)S(1)}, u32[]{:S(2)}, u32[]{:S(2)}) collective-permute-start(bf16[33,32,128]{2,1,0:T(8,128)(2,1)} %get-tuple-element.6), channel_id=1, source_target_pairs={{0,1},{1,0},{2,3},{3,2},{4,5},{5,4},{6,7},{7,6},{8,9},{9,8},{10,11... | collective-permute-start | bytes 811016 | tf_op jit(solution)/shard_map/ppermute | solution.py:379
  3.0 0.7 %collective-permute-start.1 = (bf16[33,32,128]{2,1,0:T(8,128)(2,1)}, bf16[33,32,128]{2,1,0:T(8,128)(2,1)S(1)}, u32[]{:S(2)}, u32[]{:S(2)}) collective-permute-start(bf16[33,32,128]{2,1,0:T(8,128)(2,1)} %get-tuple-element.7), channel_id=1, source_target_pairs={{1,2},{2,1},{3,4},{4,3},{5,6},{6,5},{9,10},{10,9},{11,12},{12,11},... | collective-permute-start | bytes 811016 | tf_op jit(solution)/shard_map/ppermute | solution.py:376
  3.7 2.6 %collective-permute-start.2 = (bf16[32,128]{1,0:T(8,128)(2,1)}, bf16[32,128]{1,0:T(8,128)(2,1)S(1)}, u32[]{:S(2)}, u32[]{:S(2)}) collective-permute-start(bf16[32,128]{1,0:T(8,128)(2,1)} %get-tuple-element.8), channel_id=1, source_target_pairs={{0,8},{8,0},{16,24},{24,16},{1,9},{9,1},{17,25},{25,17},{2,10},{10... | collective-permute-start | bytes 24584 | tf_op jit(solution)/shard_map/ppermute | solution.py:377
  6.3 0.6 %collective-permute-start.3 = (bf16[32,128]{1,0:T(8,128)(2,1)}, bf16[32,128]{1,0:T(8,128)(2,1)S(1)}, u32[]{:S(2)}, u32[]{:S(2)}) collective-permute-start(bf16[32,128]{1,0:T(8,128)(2,1)} %get-tuple-element.9), channel_id=1, source_target_pairs={{8,16},{16,8},{9,17},{17,9},{10,18},{18,10},{11,19},{19,11},{12,20... | collective-permute-start | bytes 24584 | tf_op jit(solution)/shard_map/ppermute | solution.py:378
  7.0 1.2 %collective-permute-done.2.xa_ref = bf16[32,128]{1,0:T(8,128)(2,1)S(1)} collective-permute-done((bf16[32,128]{1,0:T(8,128)(2,1)}, bf16[32,128]{1,0:T(8,128)(2,1)S(1)}, u32[]{:S(2)}, u32[]{:S(2)}) %collective-permute-start.2) | collective-permute-done | bytes 8224 | tf_op jit(solution)/shard_map/ppermute | solution.py:377
  8.2 0.0 collective-permute-done.3.xb_ref
  8.2 0.0 copy-start.5
  8.2 0.0 collective-permute-done.ra_ref
  8.2 0.0 copy-start.1
  8.2 0.0 collective-permute-done.1.rb_ref
  8.2 0.0 copy-start.2
  8.2 0.6 %copy-done.4 = bf16[32,128]{1,0:T(8,128)(2,1)} copy-done((bf16[32,128]{1,0:T(8,128)(2,1)}, bf16[32,128]{1,0:T(8,128)(2,1)S(1)}, u32[]{:S(2)}) %copy-start.4) | copy-done | bytes 8216
  8.8 0.0 copy-done.5
  8.8 0.1 copy-done.1
  8.9 0.1 copy-done.2
  9.0 3.8 %assemble.1 = f32[24,128]{1,0:T(8,128)} custom-call(bf16[32,32,128]{2,1,0:T(8,128)(2,1)} %f_ref.3, bf16[32,32,128]{2,1,0:T(8,128)(2,1)} %d_ref.3, bf16[33,32,128]{2,1,0:T(8,128)(2,1)} %copy-done.1, bf16[33,32,128]{2,1,0:T(8,128)(2,1)} %copy-done.2, bf16[32,128]{1,0:T(8,128)(2,1)} %copy-done.4, bf16[32,128]{1,0:T(8,128)(2,1)} %copy-done.5, s32[8,64]{1,0:T(8,128)} %bitcast.1, ...), custom_call_target="tpu_custom_call" | custom-call | tf_op jit(solution)/shard_map/assemble/pallas_call | solution.py:381
  12.8 0.7 %broadcast_in_dim.2 = f32[16,24,128]{2,1,0:T(8,128)S(1)} broadcast(f32[24,128]{1,0:T(8,128)} %assemble.1), dimensions={1,2} | broadcast | bytes 208896 | tf_op jit(solution)/shard_map/broadcast_in_dim | solution.py:396
  13.5 21.9 %all_to_all.5.mine_ref = f32[16,24,128]{2,1,0:T(8,128)S(1)} all-to-all(f32[16,24,128]{2,1,0:T(8,128)S(1)} %broadcast_in_dim.2), channel_id=1, replica_groups={{0,2,4,6,8,10,12,14,16,18,20,22,24,26,28,30},{1,3,5,7,9,11,13,15,17,19,..., dimensions={0} | all-to-all | bytes 393216 | tf_op jit(solution)/shard_map/all_to_all | solution.py:396
  35.4 0.0 collective-permute-start.4
  35.4 1.4 %collective-permute-done.4.other_ref = f32[16,24,128]{2,1,0:T(8,128)S(1)} collective-permute-done((f32[16,24,128]{2,1,0:T(8,128)S(1)}, f32[16,24,128]{2,1,0:T(8,128)S(1)}, u32[]{:S(2)}, u32[]{:S(2)}) %collective-permute-start.4) | collective-permute-done | bytes 196640 | tf_op jit(solution)/shard_map/ppermute | solution.py:397
  36.9 0.0 copy-done
  36.9 0.7 %copy-done.3 = f32[16,24,128]{2,1,0:T(8,128)} copy-done((f32[16,24,128]{2,1,0:T(8,128)}, f32[16,24,128]{2,1,0:T(8,128)S(1)}, u32[]{:S(2)}) %copy-start.3) | copy-done | bytes 196632
  37.6 4.7 %solve.1 = (f32[3,2,2,9]{3,2,1,0:T(2,128)}, f32[3,2,2,9]{3,2,1,0:T(2,128)}) custom-call(f32[16,24,128]{2,1,0:T(8,128)} %copy-done, f32[16,24,128]{2,1,0:T(8,128)} %copy-done.3), custom_call_target="tpu_custom_call" | custom-call | tf_op jit(solution)/shard_map/solve/pallas_call | solution.py:399
  (3 shorter events, 0.0 us)
Async XLA Ops:
  2.5 5.6 %collective-permute-start = (bf16[33,32,128]{2,1,0:T(8,128)(2,1)}, bf16[33,32,128]{2,1,0:T(8,128)(2,1)S(1)}, u32[]{:S(2)}, u32[]{:S(2)}) collective-permute-start(bf16[33,32,128]{2,1,0:T(8,128)(2,1)} %get-tuple-element.6), channel_id=1, source_target_pairs={{0,1},{1,0},{2,3},{3,2},{4,5},{5,4},{6,7},{7,6},{8,9},{9,8},{10,11... | collective-permute-start | bytes 811016 | tf_op jit(solution)/shard_map/ppermute | solution.py:379
  3.0 5.2 %collective-permute-start.1 = (bf16[33,32,128]{2,1,0:T(8,128)(2,1)}, bf16[33,32,128]{2,1,0:T(8,128)(2,1)S(1)}, u32[]{:S(2)}, u32[]{:S(2)}) collective-permute-start(bf16[33,32,128]{2,1,0:T(8,128)(2,1)} %get-tuple-element.7), channel_id=1, source_target_pairs={{1,2},{2,1},{3,4},{4,3},{5,6},{6,5},{9,10},{10,9},{11,12},{12,11},... | collective-permute-start | bytes 811016 | tf_op jit(solution)/shard_map/ppermute | solution.py:376
  3.7 4.5 %collective-permute-start.2 = (bf16[32,128]{1,0:T(8,128)(2,1)}, bf16[32,128]{1,0:T(8,128)(2,1)S(1)}, u32[]{:S(2)}, u32[]{:S(2)}) collective-permute-start(bf16[32,128]{1,0:T(8,128)(2,1)} %get-tuple-element.8), channel_id=1, source_target_pairs={{0,8},{8,0},{16,24},{24,16},{1,9},{9,1},{17,25},{25,17},{2,10},{10... | collective-permute-start | bytes 24584 | tf_op jit(solution)/shard_map/ppermute | solution.py:377
  6.3 1.8 %collective-permute-start.3 = (bf16[32,128]{1,0:T(8,128)(2,1)}, bf16[32,128]{1,0:T(8,128)(2,1)S(1)}, u32[]{:S(2)}, u32[]{:S(2)}) collective-permute-start(bf16[32,128]{1,0:T(8,128)(2,1)} %get-tuple-element.9), channel_id=1, source_target_pairs={{8,16},{16,8},{9,17},{17,9},{10,18},{18,10},{11,19},{19,11},{12,20... | collective-permute-start | bytes 24584 | tf_op jit(solution)/shard_map/ppermute | solution.py:378
  8.2 0.6 %copy-start.4 = (bf16[32,128]{1,0:T(8,128)(2,1)}, bf16[32,128]{1,0:T(8,128)(2,1)S(1)}, u32[]{:S(2)}) copy-start(bf16[32,128]{1,0:T(8,128)(2,1)S(1)} %collective-permute-done.2.xa_ref) | copy-start | bytes 24580
  8.2 0.6 %copy-start.5 = (bf16[32,128]{1,0:T(8,128)(2,1)}, bf16[32,128]{1,0:T(8,128)(2,1)S(1)}, u32[]{:S(2)}) copy-start(bf16[32,128]{1,0:T(8,128)(2,1)S(1)} %collective-permute-done.3.xb_ref) | copy-start | bytes 24580
  8.2 0.7 %copy-start.1 = (bf16[33,32,128]{2,1,0:T(8,128)(2,1)}, bf16[33,32,128]{2,1,0:T(8,128)(2,1)S(1)}, u32[]{:S(2)}) copy-start(bf16[33,32,128]{2,1,0:T(8,128)(2,1)S(1)} %collective-permute-done.ra_ref) | copy-start | bytes 811012
  8.2 0.8 %copy-start.2 = (bf16[33,32,128]{2,1,0:T(8,128)(2,1)}, bf16[33,32,128]{2,1,0:T(8,128)(2,1)S(1)}, u32[]{:S(2)}) copy-start(bf16[33,32,128]{2,1,0:T(8,128)(2,1)S(1)} %collective-permute-done.1.rb_ref) | copy-start | bytes 811012
  35.4 1.4 %copy-start = (f32[16,24,128]{2,1,0:T(8,128)}, f32[16,24,128]{2,1,0:T(8,128)S(1)}, u32[]{:S(2)}) copy-start(f32[16,24,128]{2,1,0:T(8,128)S(1)} %all_to_all.5.mine_ref) | copy-start | bytes 589828
  35.4 1.4 %collective-permute-start.4 = (f32[16,24,128]{2,1,0:T(8,128)S(1)}, f32[16,24,128]{2,1,0:T(8,128)S(1)}, u32[]{:S(2)}, u32[]{:S(2)}) collective-permute-start(f32[16,24,128]{2,1,0:T(8,128)S(1)} %all_to_all.5.mine_ref), channel_id=1, source_target_pairs={{0,1},{1,0},{2,3},{3,2},{4,5},{5,4},{6,7},{7,6},{8,9},{9,8},{10,11... | collective-permute-start | bytes 589832 | tf_op jit(solution)/shard_map/ppermute | solution.py:397
  36.9 0.7 %copy-start.3 = (f32[16,24,128]{2,1,0:T(8,128)}, f32[16,24,128]{2,1,0:T(8,128)S(1)}, u32[]{:S(2)}) copy-start(f32[16,24,128]{2,1,0:T(8,128)S(1)} %collective-permute-done.4.other_ref) | copy-start | bytes 589828

commit v2 on v1

--- a/solution.py
+++ b/solution.py
@@ -68,15 +68,13 @@
     return high, mid, low
 
 
-def pack_kernel(f_ref, d_ref, ya_ref, yb_ref, xa_ref, xb_ref):
+def pack_kernel(f_ref, ya_ref, yb_ref, xa_ref, xb_ref):
     even_x = lax.rem(lax.axis_index("gx"), 2) == 0
     even_y = lax.rem(lax.axis_index("gy"), 2) == 0
     bx, by, _ = f_ref.shape
-    ya_ref[0:bx] = d_ref[...]
-    yb_ref[0:bx] = d_ref[...]
     head, tail = f_ref[:, 0, :], f_ref[:, by - 1, :]
-    ya_ref[bx] = jnp.where(even_y, tail, head)
-    yb_ref[bx] = jnp.where(even_y, head, tail)
+    ya_ref[...] = jnp.where(even_y, tail, head)
+    yb_ref[...] = jnp.where(even_y, head, tail)
     xa_ref[...] = jnp.where(even_x, f_ref[bx - 1], f_ref[0])
     xb_ref[...] = jnp.where(even_x, f_ref[0], f_ref[bx - 1])
 
@@ -84,9 +82,15 @@
 PAIRS = ((0, 0), (1, 1), (2, 2), (0, 1), (1, 2), (2, 0))
 
 
-def assemble_kernel(f_ref, d_ref, ra_ref, rb_ref, xa_ref, xb_ref, col_ref, w_ref, z_ref, out_ref, field, slope, misfit, source, moment):
-    px, qy = lax.axis_index("gx"), lax.axis_index("gy")
-    even_x, even_y = lax.rem(px, 2) == 0, lax.rem(qy, 2) == 0
+def along_lanes(now, lane):
+    size = now.shape[-1]
+    up = jnp.where(lane == size - 1, 0.0, pltpu.roll(now, size - 1, 1))
+    return up - jnp.where(lane == 0, 0.0, pltpu.roll(now, 1, 1))
+
+
+def interior_kernel(f_ref, d_ref, ra_ref, rb_ref, ya_ref, yb_ref, col_ref, moment, edge, field, slope, misfit, source):
+    qy = lax.axis_index("gy")
+    even_y = lax.rem(qy, 2) == 0
     bx, by, bz = f_ref.shape
     f32 = jnp.float32
     lane = lax.broadcasted_iota(jnp.int32, (8, bz), 1)
@@ -98,37 +102,36 @@
                 at = (col_ref[qy, (i * (by // 8) + j) * 4 + k] - qy) * sign
                 code = jnp.where(lane // (bz // 4) == k, at, code)
             source[i, j * 8 : j * 8 + 8, :] = code
-    field[0, 8 : 8 + by, :] = jnp.where(even_x, xb_ref[...], xa_ref[...]).astype(f32)
-    field[bx + 1, 8 : 8 + by, :] = jnp.where(even_x, xa_ref[...], xb_ref[...]).astype(f32)
-    rim_a, rim_b = ra_ref[bx].astype(f32), rb_ref[bx].astype(f32)
-    field[1 : bx + 1, 7, :] = jnp.where(even_y, rim_b, rim_a)
-    field[1 : bx + 1, 8 + by, :] = jnp.where(even_y, rim_a, rim_b)
+    rim_a, rim_b = ya_ref[...].astype(f32), yb_ref[...].astype(f32)
+    field[:, 7, :] = jnp.where(even_y, rim_b, rim_a)
+    field[:, 8 + by, :] = jnp.where(even_y, rim_a, rim_b)
 
     def prepare(x, _):
-        here = f_ref[x].astype(f32)
-        field[x + 1, 8 : 8 + by, :] = here
-        slope[x] = field[x + 1, 9 : 9 + by, :] - field[x + 1, 7 : 7 + by, :]
+        field[x, 8 : 8 + by, :] = f_ref[x].astype(f32)
+        slope[x] = field[x, 9 : 9 + by, :] - field[x, 7 : 7 + by, :]
         code = source[x // 8]
         warped = jnp.where(code == 0, d_ref[x].astype(f32), jnp.where(code > 0, ra_ref[x].astype(f32), rb_ref[x].astype(f32)))
-        misfit[x] = here - warped
+        misfit[x] = field[x, 8 : 8 + by, :] - warped
         return 0
 
-    lax.fori_loop(0, bx, prepare, 0)
+    lax.fori_loop(0, bx, prepare, 0, unroll=4)
+    for i, x in enumerate((0, bx - 1)):
+        edge[2 * i] = slope[x]
+        edge[2 * i + 1] = misfit[x]
 
     def group(g, _):
         rows = pl.ds(pl.multiple_of(g * 8, 8), 8)
         rows_f = pl.ds(pl.multiple_of(g * 8 + 8, 8), 8)
         found = []
         for e in range(2):
-            before, now = field[e * E, rows_f, :], field[e * E + 1, rows_f, :]
+            first = e * E + (1 if e == 0 else 0)
+            last = e * E + E - (2 if e == 1 else 1)
+            before, now = field[first - 1, rows_f, :], field[first, rows_f, :]
             tot = [[jnp.zeros((8, bz), f32) for _ in range(3)] for _ in range(6)]
             right = [[jnp.zeros((8, bz), f32) for _ in range(2)] for _ in range(3)]
-            for t in range(E):
-                x = e * E + t
-                after = field[x + 2, rows_f, :]
-                up = jnp.where(lane == bz - 1, 0.0, pltpu.roll(now, bz - 1, 1))
-                down = jnp.where(lane == 0, 0.0, pltpu.roll(now, 1, 1))
-                grad = (after - before, slope[x, rows, :], up - down)
+            for x in range(first, last + 1):
+                after = field[x + 1, rows_f, :]
+                grad = (after - before, slope[x, rows, :], along_lanes(now, lane))
                 for n, (c, d) in enumerate(PAIRS):
                     tot[n][0] = tot[n][0] + grad[c] * grad[d]
                     tot[n][1] = tot[n][1] + tot[n][0]
@@ -138,6 +141,12 @@
                     right[c][0] = right[c][0] + grad[c] * miss
                     right[c][1] = right[c][1] + right[c][0]
                 before, now = now, after
+            if e == 1:
+                for n in range(6):
+                    tot[n][1] = tot[n][1] + tot[n][0]
+                    tot[n][2] = tot[n][2] + tot[n][1]
+                for c in range(3):
+                    right[c][1] = right[c][1] + right[c][0]
             ent = []
             for n in range(6):
                 a0, a1, a2 = tot[n]
@@ -163,12 +172,44 @@
 
     lax.fori_loop(0, by // 8, group, 0)
 
+
+def finish_kernel(f_ref, xa_ref, xb_ref, edge, moment, w_ref, z_ref, out_ref):
+    even_x = lax.rem(lax.axis_index("gx"), 2) == 0
+    bx, by, bz = f_ref.shape
+    f32 = jnp.float32
+    low = jnp.where(even_x, xb_ref[...], xa_ref[...]).astype(f32)
+    high = jnp.where(even_x, xa_ref[...], xb_ref[...]).astype(f32)
+    lane = lax.broadcasted_iota(jnp.int32, (by, bz), 1)
+    planes = []
+    for i, (x, before, after) in enumerate(((0, low, f_ref[1].astype(f32)), (bx - 1, f_ref[bx - 2].astype(f32), high))):
+        grad = (after - before, edge[2 * i], along_lanes(f_ref[x].astype(f32), lane))
+        planes.append(([grad[c] * grad[d] for c, d in PAIRS], [grad[c] * edge[2 * i + 1] for c in range(3)]))
     w = w_ref[...]
-    along_y = 0.0
-    for part in split3(moment[...]):
-        along_y = along_y + jnp.dot(w, part, preferred_element_type=f32)
+    along_y = []
+    for c in range(3):
+        tiles = []
+        for ix in range(3):
+            tile = moment[:, (c * 3 + ix) * bz : (c * 3 + ix + 1) * bz]
+            pieces = []
+            for s in range(2):
+                first, last = planes[0][0][s * 3 + c], planes[1][0][s * 3 + c]
+                same, cross = tile[s * 64 : s * 64 + 32], tile[s * 64 + 32 : s * 64 + 64]
+                if ix == 0:
+                    same = same + first
+                elif ix == 1:
+                    same, cross = same + last * (1 / 256), cross + last * (15 / 256)
+                else:
+                    same = same + last * (225 / 256)
+                pieces += [same, cross]
+            first, last = planes[0][1][c], planes[1][1][c]
+            pieces.append(tile[128:160] + (first, last * (1 / 16), last * (15 / 16))[ix])
+            tiles.append(jnp.concatenate(pieces, axis=0))
+        sums = 0.0
+        for part in split3(jnp.concatenate(tiles, axis=1)):
+            sums = sums + jnp.dot(w, part, preferred_element_type=f32)
+        along_y.append(sums)
     stacked = jnp.concatenate(
-        [along_y[(24 if ix == 2 else 0) : (48 if ix == 2 else 24), (c * 3 + ix) * bz : (c * 3 + ix + 1) * bz] for c in range(3) for ix in range(3)],
+        [along_y[c][(24 if ix == 2 else 0) : (48 if ix == 2 else 24), ix * bz : (ix + 1) * bz] for c in range(3) for ix in range(3)],
         axis=0,
     )
     z = z_ref[...]
@@ -176,7 +217,7 @@
     for part in split3(stacked):
         along_z = along_z + jnp.dot(part, z, preferred_element_type=f32)
 
-    slot = lane // NZN
+    slot = lax.broadcasted_iota(jnp.int32, (8, bz), 1) // NZN
     row = lax.broadcasted_iota(jnp.int32, (8, bz), 0)
     rows_out = [jnp.zeros((8, bz), f32) for _ in range(3)]
 
@@ -209,59 +250,74 @@
             for tz in range(2):
                 place(2, v0, tz, 12 + tz, row >= 4)
     for i in range(3):
-        out_ref[i * 8 : i * 8 + 8, :] = rows_out[i]
-
-
-def solve_kernel(gx, gy, mine_ref, other_ref, up_ref, res_ref, rows, table, vectors):
-    count = gx * gy
+        for copy in range(out_ref.shape[0]):
+            out_ref[copy, i * 8 : i * 8 + 8, :] = rows_out[i]
+
+
+def solve_kernel(gx, gy, mine_ref, other_ref, up_ref, res_ref, table, vectors):
+    count, half, step = gx * gy, gx * gy // 2, gy // 2
     px, qy = lax.axis_index("gx"), lax.axis_index("gy")
     odd = lax.rem(qy, 2)
     f32 = jnp.float32
-    for i in range(count // 2):
-        rows[:, 2 * i + odd, :] = mine_ref[i]
-        rows[:, 2 * i + 1 - odd, :] = other_ref[i]
     shape = (count, 128)
     lane = lax.broadcasted_iota(jnp.int32, shape, 1)
     device = lax.broadcasted_iota(jnp.int32, shape, 0)
-    q = lax.rem(device, gy)
+    core = device >= half
+    place = jnp.where(core, device - half, device)
+    chip = lax.rem(place, step)
     slot = lane // NZN
     own = lane < OWN
     ix1 = lax.rem(slot, 4) >= 2
     iy1 = lax.rem(slot, 2) == 1
     corner = own & (lax.rem(slot, 4) == 0)
-    x_low = own & ~ix1
     y_low = own & ~iy1
-    first_p, last_p = device < gy, device >= count - gy
-    first_q, last_q = q == 0, q == gy - 1
+    first_p, last_p = place < step, place >= half - step
+    first_q, last_q = (chip == 0) & ~core, (chip == step - 1) & core
+    is_odd = jnp.full((half, 128), odd, jnp.int32) == 1
+
+    def row(r):
+        a, b = mine_ref[pl.ds(r, half, stride=24), :], other_ref[pl.ds(r, half, stride=24), :]
+        return jnp.concatenate([jnp.where(is_odd, b, a), jnp.where(is_odd, a, b)], axis=0)
+
+    rows = [row(r) for r in range(24)]
 
     def lanes(value, shift):
         shift = shift % 128
         return pltpu.roll(value, shift, 1) if shift else value
 
     def down(value, shift):
-        shift = shift % count
+        shift = shift % value.shape[0]
         return pltpu.roll(value, shift, 0) if shift else value
 
+    def next_x(value, sign):
+        return down(value, -sign * step)
+
+    def next_y(value, sign):
+        low, high = value[:half], value[half:]
+        if sign > 0:
+            return jnp.concatenate([high, down(low, -1)], axis=0)
+        return jnp.concatenate([down(high, 1), low], axis=0)
+
     def from_below_x(value):
-        return jnp.where(first_p, 0.0, down(value, gy))
+        return jnp.where(first_p, 0.0, next_x(value, -1))
 
     def from_below_y(value):
-        return jnp.where(first_q, 0.0, down(value, 1))
+        return jnp.where(first_q, 0.0, next_y(value, -1))
 
     def slots(value, src, dst):
         return lanes(value, (dst - src) * NZN)
 
     def xp(v):
-        return jnp.where(ix1, down(lanes(v, 18), -gy), lanes(v, -18))
+        return jnp.where(ix1, next_x(lanes(v, 18), 1), lanes(v, -18))
 
     def xm(v):
-        return jnp.where(ix1, lanes(v, 18), down(lanes(v, -18), gy))
+        return jnp.where(ix1, lanes(v, 18), next_x(lanes(v, -18), -1))
 
     def yp(v):
-        return jnp.where(iy1, down(lanes(v, 9), -1), lanes(v, -9))
+        return jnp.where(iy1, next_y(lanes(v, 9), 1), lanes(v, -9))
 
     def ym(v):
-        return jnp.where(iy1, lanes(v, 9), down(lanes(v, -9), 1))
+        return jnp.where(iy1, lanes(v, 9), next_y(lanes(v, -9), -1))
 
     def turn(v, j):
         if j == 1:
@@ -290,18 +346,12 @@
                         entry = jnp.where(last_p & ix1, 0.0, entry)
                     if ty == 1:
                         entry = jnp.where(last_q & iy1, 0.0, entry)
-                    for dx in (1, -1) if tx else (0,):
-                        by_x = jnp.where(own, xm(entry), 0.0) if dx < 0 else entry
-                        for dy in (1, -1) if ty else (0,):
-                            by_y = jnp.where(own, ym(by_x), 0.0) if dy < 0 else by_x
-                            for dz in (1, -1) if tz else (0,):
-                                by_z = lanes(by_y, 1) if dz < 0 else by_y
-                                offset = (dx + 1) * 9 + (dy + 1) * 3 + dz + 1
-                                if s == 0:
-                                    table[offset] = by_z
-                                else:
-                                    table[54 + offset] = by_z
-                                    table[27 + offset] = turn(by_z, 2)
+                    kind = tx * 4 + ty * 2 + tz
+                    if s == 0:
+                        table[kind] = entry
+                    else:
+                        table[8 + kind] = jnp.where(own, turn(entry, 2), 0.0)
+                        table[16 + kind] = entry
 
     r0, r1, r2 = rows[20], rows[21], rows[22]
     rhs = jnp.where(iy1, lanes(r1, 9), r0) + from_below_y(jnp.where(iy1, 0.0, r2))
@@ -310,38 +360,44 @@
     rhs = jnp.where(own, rhs, 0.0)
 
     def operate(v):
-        parts = [jnp.zeros(shape, f32) for _ in range(3)]
-        for dx in range(-1, 2):
-            vx = v if dx == 0 else (xp(v) if dx > 0 else xm(v))
-            for dy in range(-1, 2):
-                vy = vx if dy == 0 else (yp(vx) if dy > 0 else ym(vx))
-                for dz in range(-1, 2):
-                    vz = lanes(vy, -dz)
-                    offset = (dx + 1) * 9 + (dy + 1) * 3 + dz + 1
-                    for s in range(3):
-                        parts[s] = parts[s] + table[27 * s + offset] * vz
+        upper = [v, lanes(v, -1)]
+        upper += [yp(u) for u in upper]
+        upper += [xp(u) for u in upper]
+        parts = []
+        for s in range(3):
+            low = []
+            for to in range(8):
+                found = 0.0
+                for up in range(8):
+                    if up & to == 0:
+                        found = found + table[8 * s + (up | to)] * upper[up]
+                low.append(found)
+            by_z = [low[2 * i] + lanes(low[2 * i + 1], 1) for i in range(4)]
+            by_y = [by_z[2 * i] + ym(by_z[2 * i + 1]) for i in range(2)]
+            parts.append(by_y[0] + xm(by_y[1]))
         coupled = parts[0] + turn(parts[1], 1) + turn(parts[2], 2)
         return damping * v + jnp.where(own, coupled, 0.0)
 
     def total(v):
         return jnp.sum(jnp.sum(v, axis=0, keepdims=True), axis=1, keepdims=True)
 
-    update = jnp.zeros(shape, f32)
-    residual = rhs
-    direction = rhs
-    norm_now = total(residual * residual)
-    for turn_at in range(ITERS):
+    def iterate(_, state):
+        update, residual, direction, norm_now = state
         image = operate(direction)
         alpha = norm_now / total(direction * image)
         update = update + alpha * direction
         residual = residual - alpha * image
-        if turn_at + 1 < ITERS:
-            norm_next = total(residual * residual)
-            direction = residual + (norm_next / norm_now) * direction
-            norm_now = norm_next
+        norm_next = total(residual * residual)
+        direction = residual + (norm_next / norm_now) * direction
+        return update, residual, direction, norm_next
+
+    start = (jnp.zeros(shape, f32), rhs, rhs, total(rhs * rhs))
+    for turn_at in range(ITERS):
+        start = iterate(turn_at, start)
+    update, residual, _, _ = start
     vectors[0] = update
     vectors[1] = residual
-    me = px * gy + qy
+    me = odd * half + px * step + qy // 2
     for i, ref in enumerate((up_ref, res_ref)):
         line = vectors[i, pl.ds(me, 1), :]
         for c in range(3):
@@ -350,6 +406,7 @@
                     ref[c, ix, iy : iy + 1, :] = lanes(line, -(c * 4 + ix * 2 + iy) * NZN)[:, :NZN]
 
 
+LIMIT = 24 * 2**20
 VMEM = pl.BlockSpec(memory_space=pltpu.VMEM)
 SMEM = pl.BlockSpec(memory_space=pltpu.SMEM)
 
@@ -366,34 +423,46 @@
     bx, by, bz = reference_scan.shape
     gx, gy = lax.axis_size("gx"), lax.axis_size("gy")
     half = jnp.bfloat16
+    rb = lax.ppermute(deformed_scan, "gy", matching("gy", 1))
+    ra = lax.ppermute(deformed_scan, "gy", matching("gy", 0))
     ya, yb, xa, xb = pl.pallas_call(
         pack_kernel,
-        out_shape=[jax.ShapeDtypeStruct((bx + 1, by, bz), half)] * 2 + [jax.ShapeDtypeStruct((by, bz), half)] * 2,
-        in_specs=[VMEM] * 2,
+        out_shape=[jax.ShapeDtypeStruct((bx, bz), half)] * 2 + [jax.ShapeDtypeStruct((by, bz), half)] * 2,
+        in_specs=[VMEM],
         out_specs=[VMEM] * 4,
+        compiler_params=pltpu.CompilerParams(vmem_limit_bytes=LIMIT),
         name="pack",
-    )(reference_scan, deformed_scan)
-    rb = lax.ppermute(yb, "gy", matching("gy", 1))
-    qa = lax.ppermute(xa, "gx", matching("gx", 0))
-    qb = lax.ppermute(xb, "gx", matching("gx", 1))
-    ra = lax.ppermute(ya, "gy", matching("gy", 0))
-    w, z = weights()
-    payload = pl.pallas_call(
-        assemble_kernel,
-        out_shape=jax.ShapeDtypeStruct((24, bz), jnp.float32),
-        in_specs=[VMEM] * 6 + [SMEM] + [VMEM] * 2,
-        out_specs=VMEM,
+    )(reference_scan)
+    yb = lax.ppermute(yb, "gy", matching("gy", 1))
+    ya = lax.ppermute(ya, "gy", matching("gy", 0))
+    xa = lax.ppermute(xa, "gx", matching("gx", 0))
+    xb = lax.ppermute(xb, "gx", matching("gx", 1))
+    moment, edge = pl.pallas_call(
+        interior_kernel,
+        out_shape=[jax.ShapeDtypeStruct((160, 9 * bz), jnp.float32), jax.ShapeDtypeStruct((4, by, bz), jnp.float32)],
+        in_specs=[VMEM] * 6 + [SMEM],
+        out_specs=[VMEM] * 2,
         scratch_shapes=[
-            pltpu.VMEM((bx + 2, by + 16, bz), jnp.float32),
+            pltpu.VMEM((bx, by + 16, bz), jnp.float32),
             pltpu.VMEM((bx, by, bz), jnp.float32),
             pltpu.VMEM((bx, by, bz), jnp.float32),
             pltpu.VMEM((bx // 8, by, bz), jnp.int32),
-            pltpu.VMEM((160, 9 * bz), jnp.float32),
         ],
-        name="assemble",
-    )(reference_scan, deformed_scan, ra, rb, qa, qb, source_column[0, :, :, 0], jnp.asarray(w, half), jnp.asarray(z, half))
+        compiler_params=pltpu.CompilerParams(vmem_limit_bytes=LIMIT),
+        cost_estimate=pl.CostEstimate(flops=8_000_000, bytes_accessed=2_000_000, transcendentals=0),
+        name="interior",
+    )(reference_scan, deformed_scan, ra, rb, ya, yb, source_column[0, :, :, 0])
+    w, z = weights()
+    payload = pl.pallas_call(
+        finish_kernel,
+        out_shape=jax.ShapeDtypeStruct((gx * gy // 2, 24, bz), jnp.float32),
+        in_specs=[VMEM] * 7,
+        out_specs=VMEM,
+        compiler_params=pltpu.CompilerParams(vmem_limit_bytes=LIMIT),
+        name="finish",
+    )(reference_scan, xa, xb, edge, moment, jnp.asarray(w, half), jnp.asarray(z, half))
     groups = [[i * 2 + core for i in range(gx * gy // 2)] for core in range(2)]
-    mine = lax.all_to_all(jnp.broadcast_to(payload[None], (gx * gy // 2, 24, bz)), ("gx", "gy"), 0, 0, axis_index_groups=groups)
+    mine = lax.all_to_all(payload, ("gx", "gy"), 0, 0, axis_index_groups=groups)
     other = lax.ppermute(mine, "gy", [(i, i ^ 1) for i in range(gy)])
     out = jax.ShapeDtypeStruct((3, 2, 2, NZN), jnp.float32)
     update, residual = pl.pallas_call(
@@ -403,11 +472,11 @@
         out_specs=[VMEM] * 2,
         scratch_shapes=[
             pltpu.VMEM((24, gx * gy, bz), jnp.float32),
-            pltpu.VMEM((81, gx * gy, bz), jnp.float32),
             pltpu.VMEM((2, gx * gy, bz), jnp.float32),
         ],
+        compiler_params=pltpu.CompilerParams(vmem_limit_bytes=LIMIT),
         name="solve",
-    )(mine, other)
+    )(mine.reshape(-1, bz), other.reshape(-1, bz))
     return update, residual
 
 

time: 42.5 us -> 35.7 us (0.84)
  Pallas kernels: 10.4 us -> 5.57 us
  starting transfers between devices: 4.44 us -> 8.08 us
  blocking collectives: 21.9 us -> 18.6 us
  local copies, waits for them, and re-layouts: 2.17 us -> 0.97 us
  waiting for transfers between devices: 2.63 us -> 1.45 us
    ppermute x4 -> x6, starting transfers between devices: 4.44 us -> 8.07 us  [the longest x1 3.91 us: local(): ya = lax.ppermute(ya, 'gy', matching('gy', 0))]
    all_to_all x1, blocking collectives: 21.9 us -> 18.6 us  [local(): mine = lax.all_to_all(payload, ('gx', 'gy'), 0, 0, axis_index_groups=groups)]
    pallas_call x2 -> x3, Pallas kernels: 5.73 us -> 2.46 us  [the longest x1 1.71 us: local(): pl.pallas_call(interior_kernel, out_shape=[jax.ShapeDtypeStruct((160, 9 *...]
    pallas_call x1, Pallas kernels: 4.68 us -> 3.11 us  [local(): pl.pallas_call(functools.partial(solve_kernel, gx, gy), out_shape=[out, o...]
    ppermute x4 -> x6, waiting for transfers between devices: 1.19 us -> 0.02 us  [the longest x1 0.01 us: local(): ya = lax.ppermute(ya, 'gy', matching('gy', 0))]
    broadcast_in_dim x1 -> x0, local copies, waits for them, and re-layouts: 0.72 us -> none  [local(): jnp.broadcast_to(payload[None], (gx * gy // 2, 24, bz))]
    unnamed x12 -> x10, local copies, waits for them, and re-layouts: 1.45 us -> 0.97 us
  transfers between devices with their start and end apart: 5 -> 7, of which waited for: 2 -> 1; matrix products, arithmetic and copies ran while one was open for 0% -> 0% of each run, Pallas kernels for 0% -> 5%
where the time goes in v2:
time: 35.7 us; the launch traced here: 35.4 us
  blocking collectives  18.6 us (52%)
  starting transfers between devices  8.08 us (23%)
  Pallas kernels  5.57 us (16%)
  waiting for transfers between devices  1.45 us (4%)
  local copies, waits for them, and re-layouts  0.97 us (3%)
  between operations  0.77 us (2%)
    all_to_all x1, blocking collectives, local(): mine = lax.all_to_all(payload, ('gx', 'gy'), 0, 0, axis_index_groups=groups)  18.6 us
    ppermute x1, starting transfers between devices, local(): ya = lax.ppermute(ya, 'gy', matching('gy', 0))  3.91 us
    pallas_call x1, Pallas kernels, local(): pl.pallas_call(functools.partial(solve_kernel, gx, gy), out_shape=[out, o...  3.11 us
    pallas_call x1, Pallas kernels, local(): pl.pallas_call(interior_kernel, out_shape=[jax.ShapeDtypeStruct((160, 9 *...  1.71 us
    ppermute x1, starting transfers between devices, local(): xa = lax.ppermute(xa, 'gx', matching('gx', 0))  1.64 us
    ppermute x1, waiting for transfers between devices, local(): other = lax.ppermute(mine, 'gy', [(i, i ^ 1) for i in range(gy)])  1.44 us
    unnamed x10, local copies, waits for them, and re-layouts  0.97 us
  transfers between devices with their start and end apart: 7, of which 1 were waited for; matrix products, arithmetic and copies ran while one was open for 0% of the time, Pallas kernels for 5%

profile of v2, /device:TPU:0, one launch (start us, length us, event | category | flops | bytes accessed | tf_op | source)
XLA Modules:
  0.0 35.4 jit_solution(2582733419864568360)
XLA Ops:
  0.6 0.6 %collective-permute-start.2 = (bf16[32,32,128]{2,1,0:T(8,128)(2,1)}, bf16[32,32,128]{2,1,0:T(8,128)(2,1)S(1)}, u32[]{:S(2)}, u32[]{:S(2)}) collective-permute-start(bf16[32,32,128]{2,1,0:T(8,128)(2,1)} %d_ref.1), channel_id=1, source_target_pairs={{0,1},{1,0},{2,3},{3,2},{4,5},{5,4},{6,7},{7,6},{8,9},{9,8},{10,11... | collective-permute-start | bytes 786440 | tf_op jit(solution)/shard_map/ppermute | solution.py:427
  1.2 0.7 %collective-permute-start.3 = (bf16[32,32,128]{2,1,0:T(8,128)(2,1)}, bf16[32,32,128]{2,1,0:T(8,128)(2,1)S(1)}, u32[]{:S(2)}, u32[]{:S(2)}) collective-permute-start(bf16[32,32,128]{2,1,0:T(8,128)(2,1)} %d_ref.1), channel_id=1, source_target_pairs={{1,2},{2,1},{3,4},{4,3},{5,6},{6,5},{9,10},{10,9},{11,12},{12,11},... | collective-permute-start | bytes 786440 | tf_op jit(solution)/shard_map/ppermute | solution.py:426
  1.9 0.0 copy-start
  1.9 0.9 %copy-done = bf16[32,32,128]{2,1,0:T(8,128)(2,1)S(1)} copy-done((bf16[32,32,128]{2,1,0:T(8,128)(2,1)S(1)}, bf16[32,32,128]{2,1,0:T(8,128)(2,1)}, u32[]{:S(2)}) %copy-start) | copy-done | bytes 262168
  2.8 0.1 pack.1
  2.9 0.0 copy-start.4
  2.9 3.9 %collective-permute-start.4 = (bf16[32,128]{1,0:T(8,128)(2,1)S(1)}, bf16[32,128]{1,0:T(8,128)(2,1)S(1)}, u32[]{:S(2)}, u32[]{:S(2)}) collective-permute-start(bf16[32,128]{1,0:T(8,128)(2,1)S(1)} %get-tuple-element.10), channel_id=1, source_target_pairs={{0,1},{1,0},{2,3},{3,2},{4,5},{5,4},{6,7},{7,6},{8,9},{9,8},{10,11... | collective-permute-start | bytes 24584 | tf_op jit(solution)/shard_map/ppermute | solution.py:437
  6.8 0.6 %collective-permute-start.5 = (bf16[32,128]{1,0:T(8,128)(2,1)S(1)}, bf16[32,128]{1,0:T(8,128)(2,1)S(1)}, u32[]{:S(2)}, u32[]{:S(2)}) collective-permute-start(bf16[32,128]{1,0:T(8,128)(2,1)S(1)} %get-tuple-element.11), channel_id=1, source_target_pairs={{1,2},{2,1},{3,4},{4,3},{5,6},{6,5},{9,10},{10,9},{11,12},{12,11},... | collective-permute-start | bytes 24584 | tf_op jit(solution)/shard_map/ppermute | solution.py:436
  7.5 1.6 %collective-permute-start = (bf16[32,128]{1,0:T(8,128)(2,1)S(1)}, bf16[32,128]{1,0:T(8,128)(2,1)S(1)}, u32[]{:S(2)}, u32[]{:S(2)}) collective-permute-start(bf16[32,128]{1,0:T(8,128)(2,1)S(1)} %get-tuple-element.8), channel_id=1, source_target_pairs={{0,8},{8,0},{16,24},{24,16},{1,9},{9,1},{17,25},{25,17},{2,10},{10... | collective-permute-start | bytes 24584 | tf_op jit(solution)/shard_map/ppermute | solution.py:438
  9.1 0.0 collective-permute-done.4.ya_ref
  9.1 0.7 %collective-permute-start.1 = (bf16[32,128]{1,0:T(8,128)(2,1)S(1)}, bf16[32,128]{1,0:T(8,128)(2,1)S(1)}, u32[]{:S(2)}, u32[]{:S(2)}) collective-permute-start(bf16[32,128]{1,0:T(8,128)(2,1)S(1)} %get-tuple-element.9), channel_id=1, source_target_pairs={{8,16},{16,8},{9,17},{17,9},{10,18},{18,10},{11,19},{19,11},{12,20... | collective-permute-start | bytes 24584 | tf_op jit(solution)/shard_map/ppermute | solution.py:439
  9.8 0.0 collective-permute-done.5.yb_ref
  9.8 0.0 collective-permute-done.2.ra_ref
  9.8 0.0 collective-permute-done.3.rb_ref
  9.8 0.0 copy-start.2
  9.8 0.0 copy-start.3
  9.8 1.7 %interior.1 = (f32[160,1152]{1,0:T(8,128)S(1)}, f32[4,32,128]{2,1,0:T(8,128)S(1)}) custom-call(bf16[32,32,128]{2,1,0:T(8,128)(2,1)S(1)} %copy-done, bf16[32,32,128]{2,1,0:T(8,128)(2,1)S(1)} %copy-done.1, bf16[32,32,128]{2,1,0:T(8,128)(2,1)S(1)} %collective-permute-done.2.ra_ref, bf16[32,32,128]{2,1,0:T(8,128)(2,1)S(1)} %collective-permute-done.3.rb_ref, ...), custom_call_target="tpu_custom_call" | custom-call | flops 8000000 | bytes 2000000 | tf_op jit(solution)/shard_map/interior/pallas_call | solution.py:440
  11.5 0.0 collective-permute-done.xa_ref
  11.6 0.0 collective-permute-done.1.xb_ref
  11.6 0.7 %finish.1 = f32[16,24,128]{2,1,0:T(8,128)S(1)} custom-call(bf16[32,32,128]{2,1,0:T(8,128)(2,1)S(1)} %copy-done, bf16[32,128]{1,0:T(8,128)(2,1)S(1)} %collective-permute-done.xa_ref, bf16[32,128]{1,0:T(8,128)(2,1)S(1)} %collective-permute-done.1.xb_ref, f32[4,32,128]{2,1,0:T(8,128)S(1)} %get-tuple-element.12.edge, f32[160,1152]{1,0:T(8,128)S(1)} %get-tuple-element.13.moment, ...), custom_call_target="tpu_custom_call" | custom-call | tf_op jit(solution)/shard_map/finish/pallas_call | solution.py:456
  12.3 18.6 %all_to_all.5 = f32[16,24,128]{2,1,0:T(8,128)S(1)} all-to-all(f32[16,24,128]{2,1,0:T(8,128)S(1)} %finish.1), channel_id=1, replica_groups={{0,2,4,6,8,10,12,14,16,18,20,22,24,26,28,30},{1,3,5,7,9,11,13,15,17,19,..., dimensions={0} | all-to-all | bytes 393216 | tf_op jit(solution)/shard_map/all_to_all | solution.py:465
  30.9 0.0 collective-permute-start.6
  30.9 1.4 %collective-permute-done.6 = f32[16,24,128]{2,1,0:T(8,128)S(1)} collective-permute-done((f32[16,24,128]{2,1,0:T(8,128)S(1)}, f32[16,24,128]{2,1,0:T(8,128)S(1)}, u32[]{:S(2)}, u32[]{:S(2)}) %collective-permute-start.6) | collective-permute-done | bytes 196640 | tf_op jit(solution)/shard_map/ppermute | solution.py:466
  32.3 3.1 %solve.1 = (f32[3,2,2,9]{3,2,1,0:T(2,128)}, f32[3,2,2,9]{3,2,1,0:T(2,128)}) custom-call(f32[384,128]{1,0:T(8,128)S(1)} %bitcast.3, f32[384,128]{1,0:T(8,128)S(1)} %bitcast.4), custom_call_target="tpu_custom_call" | custom-call | tf_op jit(solution)/shard_map/solve/pallas_call | solution.py:468
  (5 shorter events, 0.0 us)
Async XLA Ops:
  0.6 9.1 %collective-permute-start.2 = (bf16[32,32,128]{2,1,0:T(8,128)(2,1)}, bf16[32,32,128]{2,1,0:T(8,128)(2,1)S(1)}, u32[]{:S(2)}, u32[]{:S(2)}) collective-permute-start(bf16[32,32,128]{2,1,0:T(8,128)(2,1)} %d_ref.1), channel_id=1, source_target_pairs={{0,1},{1,0},{2,3},{3,2},{4,5},{5,4},{6,7},{7,6},{8,9},{9,8},{10,11... | collective-permute-start | bytes 786440 | tf_op jit(solution)/shard_map/ppermute | solution.py:427
  1.2 8.6 %collective-permute-start.3 = (bf16[32,32,128]{2,1,0:T(8,128)(2,1)}, bf16[32,32,128]{2,1,0:T(8,128)(2,1)S(1)}, u32[]{:S(2)}, u32[]{:S(2)}) collective-permute-start(bf16[32,32,128]{2,1,0:T(8,128)(2,1)} %d_ref.1), channel_id=1, source_target_pairs={{1,2},{2,1},{3,4},{4,3},{5,6},{6,5},{9,10},{10,9},{11,12},{12,11},... | collective-permute-start | bytes 786440 | tf_op jit(solution)/shard_map/ppermute | solution.py:426
  1.9 1.0 %copy-start = (bf16[32,32,128]{2,1,0:T(8,128)(2,1)S(1)}, bf16[32,32,128]{2,1,0:T(8,128)(2,1)}, u32[]{:S(2)}) copy-start(bf16[32,32,128]{2,1,0:T(8,128)(2,1)} %f_ref.5) | copy-start | bytes 786436
  2.8 7.0 %copy-start.1 = (bf16[32,32,128]{2,1,0:T(8,128)(2,1)S(1)}, bf16[32,32,128]{2,1,0:T(8,128)(2,1)}, u32[]{:S(2)}) copy-start(bf16[32,32,128]{2,1,0:T(8,128)(2,1)} %d_ref.1) | copy-start | bytes 786436
  2.9 6.9 %copy-start.4 = (s32[1,8,64,1]{2,3,1,0:T(1,128)S(1)}, s32[1,8,64,1]{2,3,1,0:T(1,128)}, u32[]{:S(2)}) copy-start(s32[1,8,64,1]{2,3,1,0:T(1,128)} %param.7) | copy-start | bytes 6148
  2.9 6.2 %collective-permute-start.4 = (bf16[32,128]{1,0:T(8,128)(2,1)S(1)}, bf16[32,128]{1,0:T(8,128)(2,1)S(1)}, u32[]{:S(2)}, u32[]{:S(2)}) collective-permute-start(bf16[32,128]{1,0:T(8,128)(2,1)S(1)} %get-tuple-element.10), channel_id=1, source_target_pairs={{0,1},{1,0},{2,3},{3,2},{4,5},{5,4},{6,7},{7,6},{8,9},{9,8},{10,11... | collective-permute-start | bytes 24584 | tf_op jit(solution)/shard_map/ppermute | solution.py:437
  6.8 3.0 %collective-permute-start.5 = (bf16[32,128]{1,0:T(8,128)(2,1)S(1)}, bf16[32,128]{1,0:T(8,128)(2,1)S(1)}, u32[]{:S(2)}, u32[]{:S(2)}) collective-permute-start(bf16[32,128]{1,0:T(8,128)(2,1)S(1)} %get-tuple-element.11), channel_id=1, source_target_pairs={{1,2},{2,1},{3,4},{4,3},{5,6},{6,5},{9,10},{10,9},{11,12},{12,11},... | collective-permute-start | bytes 24584 | tf_op jit(solution)/shard_map/ppermute | solution.py:436
  7.5 4.1 %collective-permute-start = (bf16[32,128]{1,0:T(8,128)(2,1)S(1)}, bf16[32,128]{1,0:T(8,128)(2,1)S(1)}, u32[]{:S(2)}, u32[]{:S(2)}) collective-permute-start(bf16[32,128]{1,0:T(8,128)(2,1)S(1)} %get-tuple-element.8), channel_id=1, source_target_pairs={{0,8},{8,0},{16,24},{24,16},{1,9},{9,1},{17,25},{25,17},{2,10},{10... | collective-permute-start | bytes 24584 | tf_op jit(solution)/shard_map/ppermute | solution.py:438
  9.1 2.5 %collective-permute-start.1 = (bf16[32,128]{1,0:T(8,128)(2,1)S(1)}, bf16[32,128]{1,0:T(8,128)(2,1)S(1)}, u32[]{:S(2)}, u32[]{:S(2)}) collective-permute-start(bf16[32,128]{1,0:T(8,128)(2,1)S(1)} %get-tuple-element.9), channel_id=1, source_target_pairs={{8,16},{16,8},{9,17},{17,9},{10,18},{18,10},{11,19},{19,11},{12,20... | collective-permute-start | bytes 24584 | tf_op jit(solution)/shard_map/ppermute | solution.py:439
  9.8 1.8 %copy-start.2 = (bf16[128,128]{1,0:T(8,128)(2,1)S(1)}, bf16[128,128]{1,0:T(8,128)(2,1)}, u32[]{:S(2)}) copy-start(bf16[128,128]{1,0:T(8,128)(2,1)} %constant.5.clone.z_ref) | copy-start | bytes 98308
  9.8 1.8 %copy-start.3 = (bf16[48,160]{1,0:T(8,128)(2,1)S(1)}, bf16[48,160]{1,0:T(8,128)(2,1)}, u32[]{:S(2)}) copy-start(bf16[48,160]{1,0:T(8,128)(2,1)} %constant.4.clone.w_ref) | copy-start | bytes 46084
  30.9 1.4 %collective-permute-start.6 = (f32[16,24,128]{2,1,0:T(8,128)S(1)}, f32[16,24,128]{2,1,0:T(8,128)S(1)}, u32[]{:S(2)}, u32[]{:S(2)}) collective-permute-start(f32[16,24,128]{2,1,0:T(8,128)S(1)} %all_to_all.5), channel_id=1, source_target_pairs={{0,1},{1,0},{2,3},{3,2},{4,5},{5,4},{6,7},{7,6},{8,9},{9,8},{10,11... | collective-permute-start | bytes 589832 | tf_op jit(solution)/shard_map/ppermute | solution.py:466

commit v3 on v2

--- a/solution.py
+++ b/solution.py
@@ -88,7 +88,7 @@
     return up - jnp.where(lane == 0, 0.0, pltpu.roll(now, 1, 1))
 
 
-def interior_kernel(f_ref, d_ref, ra_ref, rb_ref, ya_ref, yb_ref, col_ref, moment, edge, field, slope, misfit, source):
+def interior_kernel(gy, f_ref, d_ref, ra_ref, rb_ref, ya_ref, yb_ref, col_ref, moment, edge, field, slope, misfit, source):
     qy = lax.axis_index("gy")
     even_y = lax.rem(qy, 2) == 0
     bx, by, bz = f_ref.shape
@@ -103,8 +103,9 @@
                 code = jnp.where(lane // (bz // 4) == k, at, code)
             source[i, j * 8 : j * 8 + 8, :] = code
     rim_a, rim_b = ya_ref[...].astype(f32), yb_ref[...].astype(f32)
-    field[:, 7, :] = jnp.where(even_y, rim_b, rim_a)
-    field[:, 8 + by, :] = jnp.where(even_y, rim_a, rim_b)
+    rim_low, rim_high = jnp.where(even_y, rim_b, rim_a), jnp.where(even_y, rim_a, rim_b)
+    field[:, 7, :] = jnp.where(qy == 0, 0.0, rim_low)
+    field[:, 8 + by, :] = jnp.where(qy == gy - 1, 0.0, rim_high)
 
     def prepare(x, _):
         field[x, 8 : 8 + by, :] = f_ref[x].astype(f32)
@@ -173,12 +174,13 @@
     lax.fori_loop(0, by // 8, group, 0)
 
 
-def finish_kernel(f_ref, xa_ref, xb_ref, edge, moment, w_ref, z_ref, out_ref):
-    even_x = lax.rem(lax.axis_index("gx"), 2) == 0
+def finish_kernel(gx, f_ref, xa_ref, xb_ref, edge, moment, w_ref, z_ref, out_ref):
+    px = lax.axis_index("gx")
+    even_x = lax.rem(px, 2) == 0
     bx, by, bz = f_ref.shape
     f32 = jnp.float32
-    low = jnp.where(even_x, xb_ref[...], xa_ref[...]).astype(f32)
-    high = jnp.where(even_x, xa_ref[...], xb_ref[...]).astype(f32)
+    low = jnp.where(px == 0, 0.0, jnp.where(even_x, xb_ref[...], xa_ref[...]).astype(f32))
+    high = jnp.where(px == gx - 1, 0.0, jnp.where(even_x, xa_ref[...], xb_ref[...]).astype(f32))
     lane = lax.broadcasted_iota(jnp.int32, (by, bz), 1)
     planes = []
     for i, (x, before, after) in enumerate(((0, low, f_ref[1].astype(f32)), (bx - 1, f_ref[bx - 2].astype(f32), high))):
@@ -411,20 +413,28 @@
 SMEM = pl.BlockSpec(memory_space=pltpu.SMEM)
 
 
-def matching(axis, start):
-    count = lax.axis_size(axis)
+def exchange(value, gx, gy, axis, start):
+    def partner(p, q):
+        at, count = (p, gx) if axis == "gx" else (q, gy)
+        other = at + 1 if (at - start) % 2 == 0 else at - 1
+        if 0 <= other < count:
+            return (other, q) if axis == "gx" else (p, other)
+        return (p, q ^ 1) if axis == "gx" else (p ^ 1, q)
+
     pairs = []
-    for i in range(start, count - 1, 2):
-        pairs += [(i, i + 1), (i + 1, i)]
-    return pairs
+    for p in range(gx):
+        for q in range(gy):
+            to = partner(p, q)
+            pairs.append((p * gy + q, to[0] * gy + to[1]))
+    return lax.ppermute(value, ("gx", "gy"), pairs)
 
 
 def local(reference_scan, deformed_scan, source_column):
     bx, by, bz = reference_scan.shape
     gx, gy = lax.axis_size("gx"), lax.axis_size("gy")
     half = jnp.bfloat16
-    rb = lax.ppermute(deformed_scan, "gy", matching("gy", 1))
-    ra = lax.ppermute(deformed_scan, "gy", matching("gy", 0))
+    rb = exchange(deformed_scan, gx, gy, "gy", 1)
+    ra = exchange(deformed_scan, gx, gy, "gy", 0)
     ya, yb, xa, xb = pl.pallas_call(
         pack_kernel,
         out_shape=[jax.ShapeDtypeStruct((bx, bz), half)] * 2 + [jax.ShapeDtypeStruct((by, bz), half)] * 2,
@@ -433,12 +443,12 @@
         compiler_params=pltpu.CompilerParams(vmem_limit_bytes=LIMIT),
         name="pack",
     )(reference_scan)
-    yb = lax.ppermute(yb, "gy", matching("gy", 1))
-    ya = lax.ppermute(ya, "gy", matching("gy", 0))
-    xa = lax.ppermute(xa, "gx", matching("gx", 0))
-    xb = lax.ppermute(xb, "gx", matching("gx", 1))
+    ya = exchange(ya, gx, gy, "gy", 0)
+    xb = exchange(xb, gx, gy, "gx", 1)
+    xa = exchange(xa, gx, gy, "gx", 0)
+    yb = exchange(yb, gx, gy, "gy", 1)
     moment, edge = pl.pallas_call(
-        interior_kernel,
+        functools.partial(interior_kernel, gy),
         out_shape=[jax.ShapeDtypeStruct((160, 9 * bz), jnp.float32), jax.ShapeDtypeStruct((4, by, bz), jnp.float32)],
         in_specs=[VMEM] * 6 + [SMEM],
         out_specs=[VMEM] * 2,
@@ -454,7 +464,7 @@
     )(reference_scan, deformed_scan, ra, rb, ya, yb, source_column[0, :, :, 0])
     w, z = weights()
     payload = pl.pallas_call(
-        finish_kernel,
+        functools.partial(finish_kernel, gx),
         out_shape=jax.ShapeDtypeStruct((gx * gy // 2, 24, bz), jnp.float32),
         in_specs=[VMEM] * 7,
         out_specs=VMEM,

time: 35.7 us -> 33.8 us (0.947)
  starting transfers between devices: 8.08 us -> 6.2 us
  waiting for transfers between devices: 1.45 us -> 2.24 us
  blocking collectives: 18.6 us -> 17.9 us
    ppermute x6, starting transfers between devices: 8.07 us -> 6.19 us  [exchange(): return lax.ppermute(value, ('gx', 'gy'), pairs)]
    ppermute x6, waiting for transfers between devices: 0.02 us -> 0.8 us  [exchange(): return lax.ppermute(value, ('gx', 'gy'), pairs)]
    all_to_all x1, blocking collectives: 18.6 us -> 17.9 us  [local(): mine = lax.all_to_all(payload, ('gx', 'gy'), 0, 0, axis_index_groups=groups)]
  transfers between devices with their start and end apart: 7 -> 7, of which waited for: 1 -> 2; matrix products, arithmetic and copies ran while one was open for 0% -> 0% of each run, Pallas kernels for 5% -> 5%
where the time goes in v3:
time: 33.8 us; the launch traced here: 33.6 us
  blocking collectives  17.9 us (53%)
  starting transfers between devices  6.2 us (18%)
  Pallas kernels  5.57 us (16%)
  waiting for transfers between devices  2.24 us (7%)
  local copies, waits for them, and re-layouts  0.97 us (3%)
  between operations  0.72 us (2%)
    all_to_all x1, blocking collectives, local(): mine = lax.all_to_all(payload, ('gx', 'gy'), 0, 0, axis_index_groups=groups)  17.9 us
    ppermute x6, starting transfers between devices, exchange(): return lax.ppermute(value, ('gx', 'gy'), pairs)  6.19 us
    pallas_call x1, Pallas kernels, local(): pl.pallas_call(functools.partial(solve_kernel, gx, gy), out_shape=[out, o...  3.11 us
    pallas_call x1, Pallas kernels, local(): pl.pallas_call(functools.partial(interior_kernel, gy), out_shape=[jax.Sha...  1.71 us
    ppermute x1, waiting for transfers between devices, local(): other = lax.ppermute(mine, 'gy', [(i, i ^ 1) for i in range(gy)])  1.44 us
    unnamed x10, local copies, waits for them, and re-layouts  0.97 us
    ppermute x6, waiting for transfers between devices, exchange(): return lax.ppermute(value, ('gx', 'gy'), pairs)  0.8 us
    pallas_call x1, Pallas kernels, local(): pl.pallas_call(functools.partial(finish_kernel, gx), out_shape=jax.ShapeD...  0.69 us
  transfers between devices with their start and end apart: 7, of which 2 were waited for; matrix products, arithmetic and copies ran while one was open for 0% of the time, Pallas kernels for 5%

profile of v3, /device:TPU:0, one launch (start us, length us, event | category | flops | bytes accessed | tf_op | source)
XLA Modules:
  0.0 33.6 jit_solution(1247399124464938784)
XLA Ops:
  0.6 0.6 %collective-permute-start.2 = (bf16[32,32,128]{2,1,0:T(8,128)(2,1)}, bf16[32,32,128]{2,1,0:T(8,128)(2,1)S(1)}, u32[]{:S(2)}, u32[]{:S(2)}) collective-permute-start(bf16[32,32,128]{2,1,0:T(8,128)(2,1)} %d_ref.1), channel_id=1, source_target_pairs={{0,1},{1,0},{2,3},{3,2},{4,5},{5,4},{6,7},{7,6},{8,9},{9,8},{10,11... | collective-permute-start | bytes 786440 | tf_op jit(solution)/shard_map/ppermute | solution.py:429
  1.2 2.6 %collective-permute-start.3 = (bf16[32,32,128]{2,1,0:T(8,128)(2,1)}, bf16[32,32,128]{2,1,0:T(8,128)(2,1)S(1)}, u32[]{:S(2)}, u32[]{:S(2)}) collective-permute-start(bf16[32,32,128]{2,1,0:T(8,128)(2,1)} %d_ref.1), channel_id=1, source_target_pairs={{0,8},{1,2},{2,1},{3,4},{4,3},{5,6},{6,5},{7,15},{8,0},{9,10},{10,... | collective-permute-start | bytes 786440 | tf_op jit(solution)/shard_map/ppermute | solution.py:429
  3.8 0.9 %copy-done = bf16[32,32,128]{2,1,0:T(8,128)(2,1)S(1)} copy-done((bf16[32,32,128]{2,1,0:T(8,128)(2,1)S(1)}, bf16[32,32,128]{2,1,0:T(8,128)(2,1)}, u32[]{:S(2)}) %copy-start) | copy-done | bytes 262168
  4.8 0.1 pack.1
  4.8 0.0 copy-start.4
  4.9 0.1 collective-permute-start.4
  4.9 1.6 %collective-permute-start.5 = (bf16[32,128]{1,0:T(8,128)(2,1)S(1)}, bf16[32,128]{1,0:T(8,128)(2,1)S(1)}, u32[]{:S(2)}, u32[]{:S(2)}) collective-permute-start(bf16[32,128]{1,0:T(8,128)(2,1)S(1)} %get-tuple-element.11), channel_id=1, source_target_pairs={{0,8},{1,2},{2,1},{3,4},{4,3},{5,6},{6,5},{7,15},{8,0},{9,10},{10,... | collective-permute-start | bytes 24584 | tf_op jit(solution)/shard_map/ppermute | solution.py:429
  6.5 0.5 %collective-permute-start = (bf16[32,128]{1,0:T(8,128)(2,1)S(1)}, bf16[32,128]{1,0:T(8,128)(2,1)S(1)}, u32[]{:S(2)}, u32[]{:S(2)}) collective-permute-start(bf16[32,128]{1,0:T(8,128)(2,1)S(1)} %get-tuple-element.8), channel_id=1, source_target_pairs={{0,8},{1,9},{2,10},{3,11},{4,12},{5,13},{6,14},{7,15},{8,0},{9,1},... | collective-permute-start | bytes 24584 | tf_op jit(solution)/shard_map/ppermute | solution.py:429
  7.0 0.0 collective-permute-done.4.ya_ref
  7.0 0.8 %collective-permute-start.1 = (bf16[32,128]{1,0:T(8,128)(2,1)S(1)}, bf16[32,128]{1,0:T(8,128)(2,1)S(1)}, u32[]{:S(2)}, u32[]{:S(2)}) collective-permute-start(bf16[32,128]{1,0:T(8,128)(2,1)S(1)} %get-tuple-element.9), channel_id=1, source_target_pairs={{0,1},{1,0},{2,3},{3,2},{4,5},{5,4},{6,7},{7,6},{8,16},{9,17},{10,... | collective-permute-start | bytes 24584 | tf_op jit(solution)/shard_map/ppermute | solution.py:429
  7.9 0.8 %collective-permute-done.5.yb_ref = bf16[32,128]{1,0:T(8,128)(2,1)S(1)} collective-permute-done((bf16[32,128]{1,0:T(8,128)(2,1)S(1)}, bf16[32,128]{1,0:T(8,128)(2,1)S(1)}, u32[]{:S(2)}, u32[]{:S(2)}) %collective-permute-start.5) | collective-permute-done | bytes 8224 | tf_op jit(solution)/shard_map/ppermute | solution.py:429
  8.6 0.0 collective-permute-done.2.ra_ref
  8.7 0.0 collective-permute-done.3.rb_ref
  8.7 0.0 copy-done.1
  8.7 0.0 copy-start.2
  8.7 0.0 copy-start.3
  8.7 1.7 %interior.1 = (f32[160,1152]{1,0:T(8,128)S(1)}, f32[4,32,128]{2,1,0:T(8,128)S(1)}) custom-call(bf16[32,32,128]{2,1,0:T(8,128)(2,1)S(1)} %copy-done, bf16[32,32,128]{2,1,0:T(8,128)(2,1)S(1)} %copy-done.1, bf16[32,32,128]{2,1,0:T(8,128)(2,1)S(1)} %collective-permute-done.2.ra_ref, bf16[32,32,128]{2,1,0:T(8,128)(2,1)S(1)} %collective-permute-done.3.rb_ref, ...), custom_call_target="tpu_custom_call" | custom-call | flops 8000000 | bytes 2000000 | tf_op jit(solution)/shard_map/interior/pallas_call | solution.py:450
  10.4 0.0 collective-permute-done.xa_ref
  10.4 0.0 collective-permute-done.1.xb_ref
  10.4 0.7 %finish.1 = f32[16,24,128]{2,1,0:T(8,128)S(1)} custom-call(bf16[32,32,128]{2,1,0:T(8,128)(2,1)S(1)} %copy-done, bf16[32,128]{1,0:T(8,128)(2,1)S(1)} %collective-permute-done.xa_ref, bf16[32,128]{1,0:T(8,128)(2,1)S(1)} %collective-permute-done.1.xb_ref, f32[4,32,128]{2,1,0:T(8,128)S(1)} %get-tuple-element.12.edge, f32[160,1152]{1,0:T(8,128)S(1)} %get-tuple-element.13.moment, ...), custom_call_target="tpu_custom_call" | custom-call | tf_op jit(solution)/shard_map/finish/pallas_call | solution.py:466
  11.1 17.9 %all_to_all.5 = f32[16,24,128]{2,1,0:T(8,128)S(1)} all-to-all(f32[16,24,128]{2,1,0:T(8,128)S(1)} %finish.1), channel_id=1, replica_groups={{0,2,4,6,8,10,12,14,16,18,20,22,24,26,28,30},{1,3,5,7,9,11,13,15,17,19,..., dimensions={0} | all-to-all | bytes 393216 | tf_op jit(solution)/shard_map/all_to_all | solution.py:475
  29.0 0.0 collective-permute-start.6
  29.0 1.4 %collective-permute-done.6 = f32[16,24,128]{2,1,0:T(8,128)S(1)} collective-permute-done((f32[16,24,128]{2,1,0:T(8,128)S(1)}, f32[16,24,128]{2,1,0:T(8,128)S(1)}, u32[]{:S(2)}, u32[]{:S(2)}) %collective-permute-start.6) | collective-permute-done | bytes 196640 | tf_op jit(solution)/shard_map/ppermute | solution.py:476
  30.5 3.1 %solve.1 = (f32[3,2,2,9]{3,2,1,0:T(2,128)}, f32[3,2,2,9]{3,2,1,0:T(2,128)}) custom-call(f32[384,128]{1,0:T(8,128)S(1)} %bitcast.3, f32[384,128]{1,0:T(8,128)S(1)} %bitcast.4), custom_call_target="tpu_custom_call" | custom-call | tf_op jit(solution)/shard_map/solve/pallas_call | solution.py:478
  (5 shorter events, 0.0 us)
Async XLA Ops:
  0.6 8.0 %collective-permute-start.2 = (bf16[32,32,128]{2,1,0:T(8,128)(2,1)}, bf16[32,32,128]{2,1,0:T(8,128)(2,1)S(1)}, u32[]{:S(2)}, u32[]{:S(2)}) collective-permute-start(bf16[32,32,128]{2,1,0:T(8,128)(2,1)} %d_ref.1), channel_id=1, source_target_pairs={{0,1},{1,0},{2,3},{3,2},{4,5},{5,4},{6,7},{7,6},{8,9},{9,8},{10,11... | collective-permute-start | bytes 786440 | tf_op jit(solution)/shard_map/ppermute | solution.py:429
  1.2 7.5 %collective-permute-start.3 = (bf16[32,32,128]{2,1,0:T(8,128)(2,1)}, bf16[32,32,128]{2,1,0:T(8,128)(2,1)S(1)}, u32[]{:S(2)}, u32[]{:S(2)}) collective-permute-start(bf16[32,32,128]{2,1,0:T(8,128)(2,1)} %d_ref.1), channel_id=1, source_target_pairs={{0,8},{1,2},{2,1},{3,4},{4,3},{5,6},{6,5},{7,15},{8,0},{9,10},{10,... | collective-permute-start | bytes 786440 | tf_op jit(solution)/shard_map/ppermute | solution.py:429
  3.8 0.9 %copy-start = (bf16[32,32,128]{2,1,0:T(8,128)(2,1)S(1)}, bf16[32,32,128]{2,1,0:T(8,128)(2,1)}, u32[]{:S(2)}) copy-start(bf16[32,32,128]{2,1,0:T(8,128)(2,1)} %f_ref.5) | copy-start | bytes 786436
  4.8 3.9 %copy-start.1 = (bf16[32,32,128]{2,1,0:T(8,128)(2,1)S(1)}, bf16[32,32,128]{2,1,0:T(8,128)(2,1)}, u32[]{:S(2)}) copy-start(bf16[32,32,128]{2,1,0:T(8,128)(2,1)} %d_ref.1) | copy-start | bytes 786436
  4.8 3.8 %copy-start.4 = (s32[1,8,64,1]{2,3,1,0:T(1,128)S(1)}, s32[1,8,64,1]{2,3,1,0:T(1,128)}, u32[]{:S(2)}) copy-start(s32[1,8,64,1]{2,3,1,0:T(1,128)} %param.7) | copy-start | bytes 6148
  4.9 2.2 %collective-permute-start.4 = (bf16[32,128]{1,0:T(8,128)(2,1)S(1)}, bf16[32,128]{1,0:T(8,128)(2,1)S(1)}, u32[]{:S(2)}, u32[]{:S(2)}) collective-permute-start(bf16[32,128]{1,0:T(8,128)(2,1)S(1)} %get-tuple-element.10), channel_id=1, source_target_pairs={{0,1},{1,0},{2,3},{3,2},{4,5},{5,4},{6,7},{7,6},{8,9},{9,8},{10,11... | collective-permute-start | bytes 24584 | tf_op jit(solution)/shard_map/ppermute | solution.py:429
  4.9 3.7 %collective-permute-start.5 = (bf16[32,128]{1,0:T(8,128)(2,1)S(1)}, bf16[32,128]{1,0:T(8,128)(2,1)S(1)}, u32[]{:S(2)}, u32[]{:S(2)}) collective-permute-start(bf16[32,128]{1,0:T(8,128)(2,1)S(1)} %get-tuple-element.11), channel_id=1, source_target_pairs={{0,8},{1,2},{2,1},{3,4},{4,3},{5,6},{6,5},{7,15},{8,0},{9,10},{10,... | collective-permute-start | bytes 24584 | tf_op jit(solution)/shard_map/ppermute | solution.py:429
  6.5 3.9 %collective-permute-start = (bf16[32,128]{1,0:T(8,128)(2,1)S(1)}, bf16[32,128]{1,0:T(8,128)(2,1)S(1)}, u32[]{:S(2)}, u32[]{:S(2)}) collective-permute-start(bf16[32,128]{1,0:T(8,128)(2,1)S(1)} %get-tuple-element.8), channel_id=1, source_target_pairs={{0,8},{1,9},{2,10},{3,11},{4,12},{5,13},{6,14},{7,15},{8,0},{9,1},... | collective-permute-start | bytes 24584 | tf_op jit(solution)/shard_map/ppermute | solution.py:429
  7.0 3.4 %collective-permute-start.1 = (bf16[32,128]{1,0:T(8,128)(2,1)S(1)}, bf16[32,128]{1,0:T(8,128)(2,1)S(1)}, u32[]{:S(2)}, u32[]{:S(2)}) collective-permute-start(bf16[32,128]{1,0:T(8,128)(2,1)S(1)} %get-tuple-element.9), channel_id=1, source_target_pairs={{0,1},{1,0},{2,3},{3,2},{4,5},{5,4},{6,7},{7,6},{8,16},{9,17},{10,... | collective-permute-start | bytes 24584 | tf_op jit(solution)/shard_map/ppermute | solution.py:429
  8.7 1.8 %copy-start.2 = (bf16[128,128]{1,0:T(8,128)(2,1)S(1)}, bf16[128,128]{1,0:T(8,128)(2,1)}, u32[]{:S(2)}) copy-start(bf16[128,128]{1,0:T(8,128)(2,1)} %constant.5.clone.z_ref) | copy-start | bytes 98308
  8.7 1.8 %copy-start.3 = (bf16[48,160]{1,0:T(8,128)(2,1)S(1)}, bf16[48,160]{1,0:T(8,128)(2,1)}, u32[]{:S(2)}) copy-start(bf16[48,160]{1,0:T(8,128)(2,1)} %constant.4.clone.w_ref) | copy-start | bytes 46084
  29.0 1.4 %collective-permute-start.6 = (f32[16,24,128]{2,1,0:T(8,128)S(1)}, f32[16,24,128]{2,1,0:T(8,128)S(1)}, u32[]{:S(2)}, u32[]{:S(2)}) collective-permute-start(f32[16,24,128]{2,1,0:T(8,128)S(1)} %all_to_all.5), channel_id=1, source_target_pairs={{0,1},{1,0},{2,3},{3,2},{4,5},{5,4},{6,7},{7,6},{8,9},{9,8},{10,11... | collective-permute-start | bytes 589832 | tf_op jit(solution)/shard_map/ppermute | solution.py:476

commit v4 on v3

--- a/solution.py
+++ b/solution.py
@@ -11,6 +11,9 @@
 E = 16
 ITERS = 4
 NZN = 9
+CAP = 16
+BLOCKS = 64
+CHUNKS = 8
 OWN = 12 * NZN
 
 
@@ -68,15 +71,70 @@
     return high, mid, low
 
 
-def pack_kernel(f_ref, ya_ref, yb_ref, xa_ref, xb_ref):
+def neighbours(q, gy):
+    even = lax.rem(q, 2) == 0
+    return jnp.where(even, q + 1, q - 1), jnp.where(even, q - 1, q + 1)
+
+
+def block_lists(table, q, gy):
+    first, second = neighbours(q, gy)
+    own = table[pl.ds(q, 1), :]
+    match = [table[pl.ds(jnp.clip(to, 0, gy - 1), 1), :] == q for to in (first, second)] + [own == to for to in (first, second)]
+    match = jnp.concatenate([m.astype(jnp.float32) for m in match] * 2, axis=0).astype(jnp.bfloat16)
+    row = lax.broadcasted_iota(jnp.int32, (BLOCKS, BLOCKS), 0)
+    col = lax.broadcasted_iota(jnp.int32, (BLOCKS, BLOCKS), 1)
+
+    def against(matrix):
+        matrix = matrix.astype(jnp.float32).astype(jnp.bfloat16)
+        return lax.dot_general(matrix, match, (((1,), (1,)), ((), ())), preferred_element_type=jnp.float32)
+
+    rank, taken = against(col < row), against(col == row)
+    slot = lax.broadcasted_iota(jnp.int32, (BLOCKS, 128), 1).astype(jnp.float32)
+    number = (lax.broadcasted_iota(jnp.int32, (BLOCKS, 128), 0) + 1).astype(jnp.float32)
+    rows = []
+    for i in range(4):
+        here = (rank[:, i : i + 1] == slot) & (taken[:, i : i + 1] > 0.5)
+        rows.append(jnp.sum(jnp.where(here, number, 0.0), axis=0, keepdims=True))
+    return (jnp.concatenate(rows * 2, axis=0) - 1.0).astype(jnp.int32)
+
+
+def pack_kernel(gy, f_hbm, d_hbm, col_hbm, ya_ref, yb_ref, xa_ref, xb_ref, f_ref, d_ref, lists, col_ref, list_ref, sems, sem):
     even_x = lax.rem(lax.axis_index("gx"), 2) == 0
-    even_y = lax.rem(lax.axis_index("gy"), 2) == 0
-    bx, by, _ = f_ref.shape
-    head, tail = f_ref[:, 0, :], f_ref[:, by - 1, :]
-    ya_ref[...] = jnp.where(even_y, tail, head)
-    yb_ref[...] = jnp.where(even_y, head, tail)
-    xa_ref[...] = jnp.where(even_x, f_ref[bx - 1], f_ref[0])
-    xb_ref[...] = jnp.where(even_x, f_ref[0], f_ref[bx - 1])
+    q = lax.axis_index("gy")
+    even_y = lax.rem(q, 2) == 0
+    bx, groups, sub, bz = f_hbm.shape
+    chunk = bx // CHUNKS
+    fetch = pltpu.make_async_copy(col_hbm, col_ref, sem.at[0])
+    fetch.start()
+    copies = []
+    for n, (src, dst) in enumerate(((d_hbm, d_ref), (f_hbm, f_ref))):
+        for i in range(CHUNKS):
+            at = pl.ds(i * chunk, chunk)
+            copies.append(pltpu.make_async_copy(src.at[at], dst.at[at], sems.at[n, i]))
+            copies[-1].start()
+    fetch.wait()
+    lists[...] = block_lists(col_ref, q, gy)
+    move = pltpu.make_async_copy(lists, list_ref, sem.at[1])
+    move.start()
+    move.wait()
+    for copy in copies:
+        copy.wait()
+    quarter = lax.broadcasted_iota(jnp.int32, (64, bz), 1) // (bz // 4)
+    for n, ref in enumerate((ya_ref, yb_ref)):
+        for tile in range(CAP // 4):
+            held = jnp.zeros((64, bz), jnp.float32)
+            for k in range(4):
+                block = jnp.maximum(list_ref[n, tile * 4 + k], 0)
+                piece = d_ref[pl.ds((block >> 4) * 8, 8), (block >> 2) & 3].astype(jnp.float32).reshape(64, bz)
+                turned = pltpu.roll(piece, ((k - block) & 3) * (bz // 4), 1)
+                held = jnp.where(quarter == k, turned, held)
+            ref[tile * 8 : tile * 8 + 8] = held.astype(jnp.bfloat16).reshape(8, sub, bz)
+    head, tail = f_ref[:, 0, 0, :], f_ref[:, groups - 1, sub - 1, :]
+    ya_ref[CAP * 2 :] = jnp.where(even_y, tail, head).reshape(bx // sub, sub, bz)
+    yb_ref[CAP * 2 :] = jnp.where(even_y, head, tail).reshape(bx // sub, sub, bz)
+    first, last = f_ref[0], f_ref[bx - 1]
+    xa_ref[...] = jnp.where(even_x, last, first)
+    xb_ref[...] = jnp.where(even_x, first, last)
 
 
 PAIRS = ((0, 0), (1, 1), (2, 2), (0, 1), (1, 2), (2, 0))
@@ -88,34 +146,39 @@
     return up - jnp.where(lane == 0, 0.0, pltpu.roll(now, 1, 1))
 
 
-def interior_kernel(gy, f_ref, d_ref, ra_ref, rb_ref, ya_ref, yb_ref, col_ref, moment, edge, field, slope, misfit, source):
+def interior_kernel(gy, f_ref, d_ref, ra_ref, rb_ref, list_ref, moment, edge, field, slope, misfit):
     qy = lax.axis_index("gy")
     even_y = lax.rem(qy, 2) == 0
     bx, by, bz = f_ref.shape
     f32 = jnp.float32
     lane = lax.broadcasted_iota(jnp.int32, (8, bz), 1)
-    sign = jnp.where(even_y, 1, -1)
-    for i in range(bx // 8):
-        for j in range(by // 8):
-            code = jnp.zeros((8, bz), jnp.int32)
-            for k in range(4):
-                at = (col_ref[qy, (i * (by // 8) + j) * 4 + k] - qy) * sign
-                code = jnp.where(lane // (bz // 4) == k, at, code)
-            source[i, j * 8 : j * 8 + 8, :] = code
-    rim_a, rim_b = ya_ref[...].astype(f32), yb_ref[...].astype(f32)
+    rim_a, rim_b = (ref[CAP * 2 :].astype(f32).reshape(bx, bz) for ref in (ra_ref, rb_ref))
     rim_low, rim_high = jnp.where(even_y, rim_b, rim_a), jnp.where(even_y, rim_a, rim_b)
     field[:, 7, :] = jnp.where(qy == 0, 0.0, rim_low)
     field[:, 8 + by, :] = jnp.where(qy == gy - 1, 0.0, rim_high)
 
     def prepare(x, _):
-        field[x, 8 : 8 + by, :] = f_ref[x].astype(f32)
+        here = f_ref[x].astype(f32)
+        field[x, 8 : 8 + by, :] = here
         slope[x] = field[x, 9 : 9 + by, :] - field[x, 7 : 7 + by, :]
-        code = source[x // 8]
-        warped = jnp.where(code == 0, d_ref[x].astype(f32), jnp.where(code > 0, ra_ref[x].astype(f32), rb_ref[x].astype(f32)))
-        misfit[x] = field[x, 8 : 8 + by, :] - warped
+        misfit[x] = here - d_ref[x].astype(f32)
         return 0
 
     lax.fori_loop(0, bx, prepare, 0, unroll=4)
+    quarter = lax.broadcasted_iota(jnp.int32, (8, 8, bz), 2) // (bz // 4)
+    for n, ref in enumerate((ra_ref, rb_ref)):
+        for tile in range(CAP // 4):
+            held = ref[tile * 8 : tile * 8 + 8].astype(f32).reshape(64, bz)
+            for k in range(4):
+                listed = list_ref[2 + n, tile * 4 + k]
+                block = jnp.maximum(listed, 0)
+                turned = pltpu.roll(held, ((block - k) & 3) * (bz // 4), 1).reshape(8, 8, bz)
+                here = quarter == jnp.where(listed < 0, -1, block & 3)
+                planes = pl.ds((block >> 4) * 8, 8)
+                start = ((block >> 2) & 3) * 8
+                at = pl.ds(pl.multiple_of(start, 8), 8)
+                at_f = pl.ds(pl.multiple_of(start + 8, 8), 8)
+                misfit[planes, at, :] = jnp.where(here, field[planes, at_f, :] - turned, misfit[planes, at, :])
     for i, x in enumerate((0, bx - 1)):
         edge[2 * i] = slope[x]
         edge[2 * i + 1] = misfit[x]
@@ -409,6 +472,8 @@
 
 
 LIMIT = 24 * 2**20
+PACK_LIMIT = 55_750_000
+HBM = pl.BlockSpec(memory_space=pltpu.MemorySpace.HBM)
 VMEM = pl.BlockSpec(memory_space=pltpu.VMEM)
 SMEM = pl.BlockSpec(memory_space=pltpu.SMEM)
 
@@ -433,35 +498,45 @@
     bx, by, bz = reference_scan.shape
     gx, gy = lax.axis_size("gx"), lax.axis_size("gy")
     half = jnp.bfloat16
-    rb = exchange(deformed_scan, gx, gy, "gy", 1)
-    ra = exchange(deformed_scan, gx, gy, "gy", 0)
-    ya, yb, xa, xb = pl.pallas_call(
-        pack_kernel,
-        out_shape=[jax.ShapeDtypeStruct((bx, bz), half)] * 2 + [jax.ShapeDtypeStruct((by, bz), half)] * 2,
-        in_specs=[VMEM],
-        out_specs=[VMEM] * 4,
-        compiler_params=pltpu.CompilerParams(vmem_limit_bytes=LIMIT),
+    table = source_column[0, :, :, 0]
+    sub = 8
+    split = (bx, by // sub, sub, bz)
+    packed = jax.ShapeDtypeStruct((CAP * 2 + bx // sub, sub, bz), half)
+    plane = jax.ShapeDtypeStruct((by // sub, sub, bz), half)
+    whole = jax.ShapeDtypeStruct(split, half)
+    ya, yb, xa, xb, near, moving, lists = pl.pallas_call(
+        functools.partial(pack_kernel, gy),
+        out_shape=[packed, packed, plane, plane, whole, whole, jax.ShapeDtypeStruct((8, 128), jnp.int32)],
+        in_specs=[HBM] * 3,
+        out_specs=[VMEM] * 7,
+        scratch_shapes=[
+            pltpu.VMEM(table.shape, jnp.int32),
+            pltpu.SMEM((8, 128), jnp.int32),
+            pltpu.SemaphoreType.DMA((2, CHUNKS)),
+            pltpu.SemaphoreType.DMA((2,)),
+        ],
+        compiler_params=pltpu.CompilerParams(vmem_limit_bytes=PACK_LIMIT),
         name="pack",
-    )(reference_scan)
-    ya = exchange(ya, gx, gy, "gy", 0)
-    xb = exchange(xb, gx, gy, "gx", 1)
-    xa = exchange(xa, gx, gy, "gx", 0)
-    yb = exchange(yb, gx, gy, "gy", 1)
+    )(reference_scan.reshape(split), deformed_scan.reshape(split), table)
+    rb = exchange(yb, gx, gy, "gy", 1)
+    ra = exchange(ya, gx, gy, "gy", 0)
+    xb = exchange(xb, gx, gy, "gx", 1).reshape(by, bz)
+    xa = exchange(xa, gx, gy, "gx", 0).reshape(by, bz)
+    near, moving = near.reshape(bx, by, bz), moving.reshape(bx, by, bz)
     moment, edge = pl.pallas_call(
         functools.partial(interior_kernel, gy),
         out_shape=[jax.ShapeDtypeStruct((160, 9 * bz), jnp.float32), jax.ShapeDtypeStruct((4, by, bz), jnp.float32)],
-        in_specs=[VMEM] * 6 + [SMEM],
+        in_specs=[VMEM] * 4 + [SMEM],
         out_specs=[VMEM] * 2,
         scratch_shapes=[
             pltpu.VMEM((bx, by + 16, bz), jnp.float32),
             pltpu.VMEM((bx, by, bz), jnp.float32),
             pltpu.VMEM((bx, by, bz), jnp.float32),
-            pltpu.VMEM((bx // 8, by, bz), jnp.int32),
         ],
         compiler_params=pltpu.CompilerParams(vmem_limit_bytes=LIMIT),
         cost_estimate=pl.CostEstimate(flops=8_000_000, bytes_accessed=2_000_000, transcendentals=0),
         name="interior",
-    )(reference_scan, deformed_scan, ra, rb, ya, yb, source_column[0, :, :, 0])
+    )(near, moving, ra, rb, lists)
     w, z = weights()
     payload = pl.pallas_call(
         functools.partial(finish_kernel, gx),
@@ -470,7 +545,7 @@
         out_specs=VMEM,
         compiler_params=pltpu.CompilerParams(vmem_limit_bytes=LIMIT),
         name="finish",
-    )(reference_scan, xa, xb, edge, moment, jnp.asarray(w, half), jnp.asarray(z, half))
+    )(near, xa, xb, edge, moment, jnp.asarray(w, half), jnp.asarray(z, half))
     groups = [[i * 2 + core for i in range(gx * gy // 2)] for core in range(2)]
     mine = lax.all_to_all(payload, ("gx", "gy"), 0, 0, axis_index_groups=groups)
     other = lax.ppermute(mine, "gy", [(i, i ^ 1) for i in range(gy)])

time: 33.8 us -> 31.6 us (0.935)
  blocking collectives: 17.9 us -> 15.9 us
  starting transfers between devices: 6.2 us -> 4.52 us
  Pallas kernels: 5.57 us -> 7.05 us
    all_to_all x1, blocking collectives: 17.9 us -> 15.9 us  [local(): mine = lax.all_to_all(payload, ('gx', 'gy'), 0, 0, axis_index_groups=groups)]
    ppermute x6 -> x4, starting transfers between devices: 6.19 us -> 4.52 us  [exchange(): return lax.ppermute(value, ('gx', 'gy'), pairs)]
    pallas_call x1, Pallas kernels: 0.06 us -> 1.42 us  [local(): pl.pallas_call(functools.partial(pack_kernel, gy), out_shape=[packed, pac...]
    unnamed x10 -> x6, local copies, waits for them, and re-layouts: 0.97 us -> 0.69 us
    ppermute x6 -> x4, waiting for transfers between devices: 0.8 us -> 1.01 us  [exchange(): return lax.ppermute(value, ('gx', 'gy'), pairs)]
  transfers between devices with their start and end apart: 7 -> 5, of which waited for: 2 -> 2; matrix products, arithmetic and copies ran while one was open for 0% -> 0% of each run, Pallas kernels for 5% -> 6%
where the time goes in v4:
time: 31.6 us; the launch traced here: 31.4 us
  blocking collectives  15.9 us (50%)
  Pallas kernels  7.05 us (22%)
  starting transfers between devices  4.52 us (14%)
  waiting for transfers between devices  2.45 us (8%)
  between operations  0.7 us (2%)
  local copies, waits for them, and re-layouts  0.69 us (2%)
    all_to_all x1, blocking collectives, local(): mine = lax.all_to_all(payload, ('gx', 'gy'), 0, 0, axis_index_groups=groups)  15.9 us
    ppermute x4, starting transfers between devices, exchange(): return lax.ppermute(value, ('gx', 'gy'), pairs)  4.52 us
    pallas_call x1, Pallas kernels, local(): pl.pallas_call(functools.partial(solve_kernel, gx, gy), out_shape=[out, o...  3.11 us
    pallas_call x1, Pallas kernels, local(): pl.pallas_call(functools.partial(interior_kernel, gy), out_shape=[jax.Sha...  1.83 us
    ppermute x1, waiting for transfers between devices, local(): other = lax.ppermute(mine, 'gy', [(i, i ^ 1) for i in range(gy)])  1.44 us
    pallas_call x1, Pallas kernels, local(): pl.pallas_call(functools.partial(pack_kernel, gy), out_shape=[packed, pac...  1.42 us
    ppermute x4, waiting for transfers between devices, exchange(): return lax.ppermute(value, ('gx', 'gy'), pairs)  1.01 us
    pallas_call x1, Pallas kernels, local(): pl.pallas_call(functools.partial(finish_kernel, gx), out_shape=jax.ShapeD...  0.69 us
  transfers between devices with their start and end apart: 5, of which 2 were waited for; matrix products, arithmetic and copies ran while one was open for 0% of the time, Pallas kernels for 6%

profile of v4, /device:TPU:0, one launch (start us, length us, event | category | flops | bytes accessed | tf_op | source)
XLA Modules:
  0.0 31.4 jit_solution(6947584032583531298)
XLA Ops:
  0.6 0.0 copy-start.2
  0.6 0.7 %copy-done.2 = s32[1,8,64,1]{2,3,1,0:T(1,128)S(1)} copy-done((s32[1,8,64,1]{2,3,1,0:T(1,128)S(1)}, s32[1,8,64,1]{2,3,1,0:T(1,128)}, u32[]{:S(2)}) %copy-start.2) | copy-done | bytes 2072
  1.3 1.4 %pack.1 = (bf16[36,8,128]{2,1,0:T(8,128)(2,1)S(1)}, bf16[36,8,128]{2,1,0:T(8,128)(2,1)S(1)}, bf16[4,8,128]{2,1,0:T(8,128)(2,1)S(1)}, bf16[4,8,128]{2,1,0:T(8,128...) custom-call(bf16[32,4,8,128]{3,2,1,0:T(8,128)(2,1)} %bitcast.17, ...), custom_call_target="tpu_custom_call" | custom-call | tf_op jit(solution)/shard_map/pack/pallas_call | solution.py:507
  2.7 0.6 %collective-permute-start.2 = (bf16[36,8,128]{2,1,0:T(8,128)(2,1)S(1)}, bf16[36,8,128]{2,1,0:T(8,128)(2,1)S(1)}, u32[]{:S(2)}, u32[]{:S(2)}) collective-permute-start(bf16[36,8,128]{2,1,0:T(8,128)(2,1)S(1)} %get-tuple-element.15), channel_id=1, source_target_pairs={{0,1},{1,0},{2,3},{3,2},{4,5},{5,4},{6,7},{7,6},{8,9},{9,8},{10,11... | collective-permute-start | bytes 221192 | tf_op jit(solution)/shard_map/ppermute | solution.py:494
  3.3 2.6 %collective-permute-start.3 = (bf16[36,8,128]{2,1,0:T(8,128)(2,1)S(1)}, bf16[36,8,128]{2,1,0:T(8,128)(2,1)S(1)}, u32[]{:S(2)}, u32[]{:S(2)}) collective-permute-start(bf16[36,8,128]{2,1,0:T(8,128)(2,1)S(1)} %get-tuple-element.16), channel_id=1, source_target_pairs={{0,8},{1,2},{2,1},{3,4},{4,3},{5,6},{6,5},{7,15},{8,0},{9,10},{10,... | collective-permute-start | bytes 221192 | tf_op jit(solution)/shard_map/ppermute | solution.py:494
  5.9 0.1 collective-permute-start
  6.0 1.2 %collective-permute-start.1 = (bf16[4,8,128]{2,1,0:T(8,128)(2,1)S(1)}, bf16[4,8,128]{2,1,0:T(8,128)(2,1)S(1)}, u32[]{:S(2)}, u32[]{:S(2)}) collective-permute-start(bf16[4,8,128]{2,1,0:T(8,128)(2,1)S(1)} %get-tuple-element.13), channel_id=1, source_target_pairs={{0,1},{1,0},{2,3},{3,2},{4,5},{5,4},{6,7},{7,6},{8,16},{9,17},{10,... | collective-permute-start | bytes 24584 | tf_op jit(solution)/shard_map/ppermute | solution.py:494
  7.3 0.0 collective-permute-done.2.ra_ref
  7.3 1.0 %collective-permute-done.3.rb_ref = bf16[36,8,128]{2,1,0:T(8,128)(2,1)S(1)} collective-permute-done((bf16[36,8,128]{2,1,0:T(8,128)(2,1)S(1)}, bf16[36,8,128]{2,1,0:T(8,128)(2,1)S(1)}, u32[]{:S(2)}, u32[]{:S(2)}) %collective-permute-start.3) | collective-permute-done | bytes 73760 | tf_op jit(solution)/shard_map/ppermute | solution.py:494
  8.3 0.0 copy-start
  8.3 0.0 copy-start.1
  8.3 1.8 %interior.1 = (f32[160,1152]{1,0:T(8,128)S(1)}, f32[4,32,128]{2,1,0:T(8,128)S(1)}) custom-call(bf16[32,32,128]{2,1,0:T(8,128)(2,1)S(1)} %bitcast.9, bf16[32,32,128]{2,1,0:T(8,128)(2,1)S(1)} %bitcast.12, bf16[36,8,128]{2,1,0:T(8,128)(2,1)S(1)} %collective-permute-done.2.ra_ref, bf16[36,8,128]{2,1,0:T(8,128)(2,1)S(1)} %collective-permute-done.3.rb_ref, ...), custom_call_target="tpu_custom_call" | custom-call | flops 8000000 | bytes 2000000 | tf_op jit(solution)/shard_map/interior/pallas_call | solution.py:526
  10.1 0.0 collective-permute-done
  10.1 0.0 collective-permute-done.1
  10.1 0.0 copy-done
  10.1 0.0 copy-done.1
  10.2 0.7 %finish.1 = f32[16,24,128]{2,1,0:T(8,128)S(1)} custom-call(bf16[32,32,128]{2,1,0:T(8,128)(2,1)S(1)} %bitcast.10, bf16[32,128]{1,0:T(8,128)(2,1)S(1)} %bitcast.14, bf16[32,128]{1,0:T(8,128)(2,1)S(1)} %bitcast.15, f32[4,32,128]{2,1,0:T(8,128)S(1)} %get-tuple-element.18.edge, f32[160,1152]{1,0:T(8,128)S(1)} %get-tuple-element.19.moment, ...), custom_call_target="tpu_custom_call" | custom-call | tf_op jit(solution)/shard_map/finish/pallas_call | solution.py:541
  10.9 15.9 %all_to_all.5 = f32[16,24,128]{2,1,0:T(8,128)S(1)} all-to-all(f32[16,24,128]{2,1,0:T(8,128)S(1)} %finish.1), channel_id=1, replica_groups={{0,2,4,6,8,10,12,14,16,18,20,22,24,26,28,30},{1,3,5,7,9,11,13,15,17,19,..., dimensions={0} | all-to-all | bytes 393216 | tf_op jit(solution)/shard_map/all_to_all | solution.py:550
  26.8 0.0 collective-permute-start.4
  26.8 1.4 %collective-permute-done.4 = f32[16,24,128]{2,1,0:T(8,128)S(1)} collective-permute-done((f32[16,24,128]{2,1,0:T(8,128)S(1)}, f32[16,24,128]{2,1,0:T(8,128)S(1)}, u32[]{:S(2)}, u32[]{:S(2)}) %collective-permute-start.4) | collective-permute-done | bytes 196640 | tf_op jit(solution)/shard_map/ppermute | solution.py:551
  28.2 3.1 %solve.1 = (f32[3,2,2,9]{3,2,1,0:T(2,128)}, f32[3,2,2,9]{3,2,1,0:T(2,128)}) custom-call(f32[384,128]{1,0:T(8,128)S(1)} %bitcast.11, f32[384,128]{1,0:T(8,128)S(1)} %bitcast.13), custom_call_target="tpu_custom_call" | custom-call | tf_op jit(solution)/shard_map/solve/pallas_call | solution.py:553
Async XLA Ops:
  0.6 0.7 %copy-start.2 = (s32[1,8,64,1]{2,3,1,0:T(1,128)S(1)}, s32[1,8,64,1]{2,3,1,0:T(1,128)}, u32[]{:S(2)}) copy-start(s32[1,8,64,1]{2,3,1,0:T(1,128)} %param.7) | copy-start | bytes 6148
  2.7 4.5 %collective-permute-start.2 = (bf16[36,8,128]{2,1,0:T(8,128)(2,1)S(1)}, bf16[36,8,128]{2,1,0:T(8,128)(2,1)S(1)}, u32[]{:S(2)}, u32[]{:S(2)}) collective-permute-start(bf16[36,8,128]{2,1,0:T(8,128)(2,1)S(1)} %get-tuple-element.15), channel_id=1, source_target_pairs={{0,1},{1,0},{2,3},{3,2},{4,5},{5,4},{6,7},{7,6},{8,9},{9,8},{10,11... | collective-permute-start | bytes 221192 | tf_op jit(solution)/shard_map/ppermute | solution.py:494
  3.3 5.0 %collective-permute-start.3 = (bf16[36,8,128]{2,1,0:T(8,128)(2,1)S(1)}, bf16[36,8,128]{2,1,0:T(8,128)(2,1)S(1)}, u32[]{:S(2)}, u32[]{:S(2)}) collective-permute-start(bf16[36,8,128]{2,1,0:T(8,128)(2,1)S(1)} %get-tuple-element.16), channel_id=1, source_target_pairs={{0,8},{1,2},{2,1},{3,4},{4,3},{5,6},{6,5},{7,15},{8,0},{9,10},{10,... | collective-permute-start | bytes 221192 | tf_op jit(solution)/shard_map/ppermute | solution.py:494
  5.9 4.2 %collective-permute-start = (bf16[4,8,128]{2,1,0:T(8,128)(2,1)S(1)}, bf16[4,8,128]{2,1,0:T(8,128)(2,1)S(1)}, u32[]{:S(2)}, u32[]{:S(2)}) collective-permute-start(bf16[4,8,128]{2,1,0:T(8,128)(2,1)S(1)} %get-tuple-element.12), channel_id=1, source_target_pairs={{0,8},{1,9},{2,10},{3,11},{4,12},{5,13},{6,14},{7,15},{8,0},{9,1},... | collective-permute-start | bytes 24584 | tf_op jit(solution)/shard_map/ppermute | solution.py:494
  6.0 4.1 %collective-permute-start.1 = (bf16[4,8,128]{2,1,0:T(8,128)(2,1)S(1)}, bf16[4,8,128]{2,1,0:T(8,128)(2,1)S(1)}, u32[]{:S(2)}, u32[]{:S(2)}) collective-permute-start(bf16[4,8,128]{2,1,0:T(8,128)(2,1)S(1)} %get-tuple-element.13), channel_id=1, source_target_pairs={{0,1},{1,0},{2,3},{3,2},{4,5},{5,4},{6,7},{7,6},{8,16},{9,17},{10,... | collective-permute-start | bytes 24584 | tf_op jit(solution)/shard_map/ppermute | solution.py:494
  8.3 1.9 %copy-start = (bf16[128,128]{1,0:T(8,128)(2,1)S(1)}, bf16[128,128]{1,0:T(8,128)(2,1)}, u32[]{:S(2)}) copy-start(bf16[128,128]{1,0:T(8,128)(2,1)} %constant.5.clone.z_ref) | copy-start | bytes 98308
  8.3 1.9 %copy-start.1 = (bf16[48,160]{1,0:T(8,128)(2,1)S(1)}, bf16[48,160]{1,0:T(8,128)(2,1)}, u32[]{:S(2)}) copy-start(bf16[48,160]{1,0:T(8,128)(2,1)} %constant.4.clone.w_ref) | copy-start | bytes 46084
  26.8 1.4 %collective-permute-start.4 = (f32[16,24,128]{2,1,0:T(8,128)S(1)}, f32[16,24,128]{2,1,0:T(8,128)S(1)}, u32[]{:S(2)}, u32[]{:S(2)}) collective-permute-start(f32[16,24,128]{2,1,0:T(8,128)S(1)} %all_to_all.5), channel_id=1, source_target_pairs={{0,1},{1,0},{2,3},{3,2},{4,5},{5,4},{6,7},{7,6},{8,9},{9,8},{10,11... | collective-permute-start | bytes 589832 | tf_op jit(solution)/shard_map/ppermute | solution.py:551

commit v5 on v4

--- a/solution.py
+++ b/solution.py
@@ -8,12 +8,13 @@
 from jax.experimental.pallas import tpu as pltpu
 from jax.sharding import PartitionSpec as P
 
+
 E = 16
 ITERS = 4
 NZN = 9
 CAP = 16
 BLOCKS = 64
-CHUNKS = 8
+CHUNKS = 2
 OWN = 12 * NZN
 
 
@@ -71,13 +72,13 @@
     return high, mid, low
 
 
-def neighbours(q, gy):
+def neighbours(q):
     even = lax.rem(q, 2) == 0
     return jnp.where(even, q + 1, q - 1), jnp.where(even, q - 1, q + 1)
 
 
 def block_lists(table, q, gy):
-    first, second = neighbours(q, gy)
+    first, second = neighbours(q)
     own = table[pl.ds(q, 1), :]
     match = [table[pl.ds(jnp.clip(to, 0, gy - 1), 1), :] == q for to in (first, second)] + [own == to for to in (first, second)]
     match = jnp.concatenate([m.astype(jnp.float32) for m in match] * 2, axis=0).astype(jnp.bfloat16)
@@ -98,37 +99,40 @@
     return (jnp.concatenate(rows * 2, axis=0) - 1.0).astype(jnp.int32)
 
 
-def pack_kernel(gy, f_hbm, d_hbm, col_hbm, ya_ref, yb_ref, xa_ref, xb_ref, f_ref, d_ref, lists, col_ref, list_ref, sems, sem):
+def pack_kernel(gy, f_hbm, d_hbm, col_hbm, ya_ref, yb_ref, xa_ref, xb_ref, f_ref, d_ref, lists, col_ref, sems, sem):
     even_x = lax.rem(lax.axis_index("gx"), 2) == 0
     q = lax.axis_index("gy")
     even_y = lax.rem(q, 2) == 0
     bx, groups, sub, bz = f_hbm.shape
     chunk = bx // CHUNKS
-    fetch = pltpu.make_async_copy(col_hbm, col_ref, sem.at[0])
+    fetch = pltpu.make_async_copy(col_hbm, col_ref, sem)
     fetch.start()
     copies = []
     for n, (src, dst) in enumerate(((d_hbm, d_ref), (f_hbm, f_ref))):
         for i in range(CHUNKS):
             at = pl.ds(i * chunk, chunk)
             copies.append(pltpu.make_async_copy(src.at[at], dst.at[at], sems.at[n, i]))
-            copies[-1].start()
+    for copy in copies[:CHUNKS]:
+        copy.start()
     fetch.wait()
-    lists[...] = block_lists(col_ref, q, gy)
-    move = pltpu.make_async_copy(lists, list_ref, sem.at[1])
-    move.start()
-    move.wait()
-    for copy in copies:
+    found = block_lists(col_ref, q, gy)
+    lists[...] = found
+    for copy in copies[CHUNKS:]:
+        copy.start()
+    for copy in copies[:CHUNKS]:
         copy.wait()
     quarter = lax.broadcasted_iota(jnp.int32, (64, bz), 1) // (bz // 4)
     for n, ref in enumerate((ya_ref, yb_ref)):
         for tile in range(CAP // 4):
             held = jnp.zeros((64, bz), jnp.float32)
             for k in range(4):
-                block = jnp.maximum(list_ref[n, tile * 4 + k], 0)
+                block = jnp.maximum(found[n, tile * 4 + k], 0)
                 piece = d_ref[pl.ds((block >> 4) * 8, 8), (block >> 2) & 3].astype(jnp.float32).reshape(64, bz)
                 turned = pltpu.roll(piece, ((k - block) & 3) * (bz // 4), 1)
                 held = jnp.where(quarter == k, turned, held)
             ref[tile * 8 : tile * 8 + 8] = held.astype(jnp.bfloat16).reshape(8, sub, bz)
+    for copy in copies[CHUNKS:]:
+        copy.wait()
     head, tail = f_ref[:, 0, 0, :], f_ref[:, groups - 1, sub - 1, :]
     ya_ref[CAP * 2 :] = jnp.where(even_y, tail, head).reshape(bx // sub, sub, bz)
     yb_ref[CAP * 2 :] = jnp.where(even_y, head, tail).reshape(bx // sub, sub, bz)
@@ -146,7 +150,9 @@
     return up - jnp.where(lane == 0, 0.0, pltpu.roll(now, 1, 1))
 
 
-def interior_kernel(gy, f_ref, d_ref, ra_ref, rb_ref, list_ref, moment, edge, field, slope, misfit):
+def interior_kernel(gy, f_ref, d_ref, ra_ref, rb_ref, lists, moment, edge, field, slope, misfit, list_ref, sem):
+    move = pltpu.make_async_copy(lists, list_ref, sem)
+    move.start()
     qy = lax.axis_index("gy")
     even_y = lax.rem(qy, 2) == 0
     bx, by, bz = f_ref.shape
@@ -165,6 +171,7 @@
         return 0
 
     lax.fori_loop(0, bx, prepare, 0, unroll=4)
+    move.wait()
     quarter = lax.broadcasted_iota(jnp.int32, (8, 8, bz), 2) // (bz // 4)
     for n, ref in enumerate((ra_ref, rb_ref)):
         for tile in range(CAP // 4):
@@ -446,7 +453,7 @@
     def total(v):
         return jnp.sum(jnp.sum(v, axis=0, keepdims=True), axis=1, keepdims=True)
 
-    def iterate(_, state):
+    def iterate(state):
         update, residual, direction, norm_now = state
         image = operate(direction)
         alpha = norm_now / total(direction * image)
@@ -457,8 +464,8 @@
         return update, residual, direction, norm_next
 
     start = (jnp.zeros(shape, f32), rhs, rhs, total(rhs * rhs))
-    for turn_at in range(ITERS):
-        start = iterate(turn_at, start)
+    for _ in range(ITERS):
+        start = iterate(start)
     update, residual, _, _ = start
     vectors[0] = update
     vectors[1] = residual
@@ -472,10 +479,8 @@
 
 
 LIMIT = 24 * 2**20
-PACK_LIMIT = 55_750_000
 HBM = pl.BlockSpec(memory_space=pltpu.MemorySpace.HBM)
 VMEM = pl.BlockSpec(memory_space=pltpu.VMEM)
-SMEM = pl.BlockSpec(memory_space=pltpu.SMEM)
 
 
 def exchange(value, gx, gy, axis, start):
@@ -511,27 +516,29 @@
         out_specs=[VMEM] * 7,
         scratch_shapes=[
             pltpu.VMEM(table.shape, jnp.int32),
-            pltpu.SMEM((8, 128), jnp.int32),
             pltpu.SemaphoreType.DMA((2, CHUNKS)),
-            pltpu.SemaphoreType.DMA((2,)),
+            pltpu.SemaphoreType.DMA,
         ],
-        compiler_params=pltpu.CompilerParams(vmem_limit_bytes=PACK_LIMIT),
+        compiler_params=pltpu.CompilerParams(vmem_limit_bytes=LIMIT),
         name="pack",
-    )(reference_scan.reshape(split), deformed_scan.reshape(split), table)
+    )(*(pltpu.with_memory_space_constraint(value, pltpu.MemorySpace.HBM) for value in (reference_scan.reshape(split), deformed_scan.reshape(split), table)))
     rb = exchange(yb, gx, gy, "gy", 1)
+    xb = exchange(xb, gx, gy, "gx", 1)
+    xa = exchange(xa, gx, gy, "gx", 0)
     ra = exchange(ya, gx, gy, "gy", 0)
-    xb = exchange(xb, gx, gy, "gx", 1).reshape(by, bz)
-    xa = exchange(xa, gx, gy, "gx", 0).reshape(by, bz)
+    xa, xb = xa.reshape(by, bz), xb.reshape(by, bz)
     near, moving = near.reshape(bx, by, bz), moving.reshape(bx, by, bz)
     moment, edge = pl.pallas_call(
         functools.partial(interior_kernel, gy),
         out_shape=[jax.ShapeDtypeStruct((160, 9 * bz), jnp.float32), jax.ShapeDtypeStruct((4, by, bz), jnp.float32)],
-        in_specs=[VMEM] * 4 + [SMEM],
+        in_specs=[VMEM] * 5,
         out_specs=[VMEM] * 2,
         scratch_shapes=[
             pltpu.VMEM((bx, by + 16, bz), jnp.float32),
             pltpu.VMEM((bx, by, bz), jnp.float32),
             pltpu.VMEM((bx, by, bz), jnp.float32),
+            pltpu.SMEM((8, 128), jnp.int32),
+            pltpu.SemaphoreType.DMA,
         ],
         compiler_params=pltpu.CompilerParams(vmem_limit_bytes=LIMIT),
         cost_estimate=pl.CostEstimate(flops=8_000_000, bytes_accessed=2_000_000, transcendentals=0),

time: 31.6 us -> 31.1 us (0.984)
  local copies, waits for them, and re-layouts: 0.69 us -> 0.01 us
    unnamed x6 -> x4, local copies, waits for them, and re-layouts: 0.69 us -> 0.01 us
    pallas_call x1, Pallas kernels: 1.42 us -> 1.86 us  [local(): pl.pallas_call(functools.partial(pack_kernel, gy), out_shape=[packed, pac...]
  transfers between devices with their start and end apart: 5 -> 5, of which waited for: 2 -> 2; matrix products, arithmetic and copies ran while one was open for 0% -> 0% of each run, Pallas kernels for 6% -> 5%
where the time goes in v5:
time: 31.1 us; the launch traced here: 30.9 us
  blocking collectives  15.9 us (51%)
  Pallas kernels  7.32 us (24%)
  starting transfers between devices  4.52 us (15%)
  waiting for transfers between devices  2.45 us (8%)
  between operations  0.69 us (2%)
    all_to_all x1, blocking collectives, local(): mine = lax.all_to_all(payload, ('gx', 'gy'), 0, 0, axis_index_groups=groups)  15.9 us
    ppermute x4, starting transfers between devices, exchange(): return lax.ppermute(value, ('gx', 'gy'), pairs)  4.52 us
    pallas_call x1, Pallas kernels, local(): pl.pallas_call(functools.partial(solve_kernel, gx, gy), out_shape=[out, o...  3.11 us
    pallas_call x1, Pallas kernels, local(): pl.pallas_call(functools.partial(pack_kernel, gy), out_shape=[packed, pac...  1.86 us
    pallas_call x1, Pallas kernels, local(): pl.pallas_call(functools.partial(interior_kernel, gy), out_shape=[jax.Sha...  1.66 us
    ppermute x1, waiting for transfers between devices, local(): other = lax.ppermute(mine, 'gy', [(i, i ^ 1) for i in range(gy)])  1.44 us
    ppermute x4, waiting for transfers between devices, exchange(): return lax.ppermute(value, ('gx', 'gy'), pairs)  1.01 us
    pallas_call x1, Pallas kernels, local(): pl.pallas_call(functools.partial(finish_kernel, gx), out_shape=jax.ShapeD...  0.69 us
  transfers between devices with their start and end apart: 5, of which 2 were waited for; matrix products, arithmetic and copies ran while one was open for 0% of the time, Pallas kernels for 5%

profile of v5, /device:TPU:0, one launch (start us, length us, event | category | flops | bytes accessed | tf_op | source)
XLA Modules:
  0.0 30.9 jit_solution(17918541236224296982)
XLA Ops:
  0.6 1.9 %pack.1 = (bf16[36,8,128]{2,1,0:T(8,128)(2,1)S(1)}, bf16[36,8,128]{2,1,0:T(8,128)(2,1)S(1)}, bf16[4,8,128]{2,1,0:T(8,128)(2,1)S(1)}, bf16[4,8,128]{2,1,0:T(8,128...) custom-call(bf16[32,4,8,128]{3,2,1,0:T(8,128)(2,1)} %bitcast.16, ...), custom_call_target="tpu_custom_call" | custom-call | tf_op jit(solution)/shard_map/pack/pallas_call | solution.py:512
  2.5 0.6 %collective-permute-start.2 = (bf16[36,8,128]{2,1,0:T(8,128)(2,1)S(1)}, bf16[36,8,128]{2,1,0:T(8,128)(2,1)S(1)}, u32[]{:S(2)}, u32[]{:S(2)}) collective-permute-start(bf16[36,8,128]{2,1,0:T(8,128)(2,1)S(1)} %get-tuple-element.15), channel_id=1, source_target_pairs={{0,1},{1,0},{2,3},{3,2},{4,5},{5,4},{6,7},{7,6},{8,9},{9,8},{10,11... | collective-permute-start | bytes 221192 | tf_op jit(solution)/shard_map/ppermute | solution.py:499
  3.1 2.6 %collective-permute-start.3 = (bf16[36,8,128]{2,1,0:T(8,128)(2,1)S(1)}, bf16[36,8,128]{2,1,0:T(8,128)(2,1)S(1)}, u32[]{:S(2)}, u32[]{:S(2)}) collective-permute-start(bf16[36,8,128]{2,1,0:T(8,128)(2,1)S(1)} %get-tuple-element.16), channel_id=1, source_target_pairs={{0,8},{1,2},{2,1},{3,4},{4,3},{5,6},{6,5},{7,15},{8,0},{9,10},{10,... | collective-permute-start | bytes 221192 | tf_op jit(solution)/shard_map/ppermute | solution.py:499
  5.7 0.1 collective-permute-start
  5.8 1.2 %collective-permute-start.1 = (bf16[4,8,128]{2,1,0:T(8,128)(2,1)S(1)}, bf16[4,8,128]{2,1,0:T(8,128)(2,1)S(1)}, u32[]{:S(2)}, u32[]{:S(2)}) collective-permute-start(bf16[4,8,128]{2,1,0:T(8,128)(2,1)S(1)} %get-tuple-element.13), channel_id=1, source_target_pairs={{0,1},{1,0},{2,3},{3,2},{4,5},{5,4},{6,7},{7,6},{8,16},{9,17},{10,... | collective-permute-start | bytes 24584 | tf_op jit(solution)/shard_map/ppermute | solution.py:499
  7.0 0.0 collective-permute-done.2.ra_ref
  7.0 1.0 %collective-permute-done.3.rb_ref = bf16[36,8,128]{2,1,0:T(8,128)(2,1)S(1)} collective-permute-done((bf16[36,8,128]{2,1,0:T(8,128)(2,1)S(1)}, bf16[36,8,128]{2,1,0:T(8,128)(2,1)S(1)}, u32[]{:S(2)}, u32[]{:S(2)}) %collective-permute-start.3) | collective-permute-done | bytes 73760 | tf_op jit(solution)/shard_map/ppermute | solution.py:499
  8.0 0.0 copy-start
  8.0 0.0 copy-start.1
  8.0 1.7 %interior.1 = (f32[160,1152]{1,0:T(8,128)S(1)}, f32[4,32,128]{2,1,0:T(8,128)S(1)}) custom-call(bf16[32,32,128]{2,1,0:T(8,128)(2,1)S(1)} %bitcast.9, bf16[32,32,128]{2,1,0:T(8,128)(2,1)S(1)} %bitcast.12, bf16[36,8,128]{2,1,0:T(8,128)(2,1)S(1)} %collective-permute-done.2.ra_ref, bf16[36,8,128]{2,1,0:T(8,128)(2,1)S(1)} %collective-permute-done.3.rb_ref, ...), custom_call_target="tpu_custom_call" | custom-call | flops 8000000 | bytes 2000000 | tf_op jit(solution)/shard_map/interior/pallas_call | solution.py:531
  9.7 0.0 collective-permute-done
  9.7 0.0 collective-permute-done.1
  9.7 0.0 copy-done
  9.7 0.0 copy-done.1
  9.7 0.7 %finish.1 = f32[16,24,128]{2,1,0:T(8,128)S(1)} custom-call(bf16[32,32,128]{2,1,0:T(8,128)(2,1)S(1)} %bitcast.10, bf16[32,128]{1,0:T(8,128)(2,1)S(1)} %bitcast.14, bf16[32,128]{1,0:T(8,128)(2,1)S(1)} %bitcast.15, f32[4,32,128]{2,1,0:T(8,128)S(1)} %get-tuple-element.18.edge, f32[160,1152]{1,0:T(8,128)S(1)} %get-tuple-element.19.moment, ...), custom_call_target="tpu_custom_call" | custom-call | tf_op jit(solution)/shard_map/finish/pallas_call | solution.py:548
  10.4 15.9 %all_to_all.5 = f32[16,24,128]{2,1,0:T(8,128)S(1)} all-to-all(f32[16,24,128]{2,1,0:T(8,128)S(1)} %finish.1), channel_id=1, replica_groups={{0,2,4,6,8,10,12,14,16,18,20,22,24,26,28,30},{1,3,5,7,9,11,13,15,17,19,..., dimensions={0} | all-to-all | bytes 393216 | tf_op jit(solution)/shard_map/all_to_all | solution.py:557
  26.4 0.0 collective-permute-start.4
  26.4 1.4 %collective-permute-done.4 = f32[16,24,128]{2,1,0:T(8,128)S(1)} collective-permute-done((f32[16,24,128]{2,1,0:T(8,128)S(1)}, f32[16,24,128]{2,1,0:T(8,128)S(1)}, u32[]{:S(2)}, u32[]{:S(2)}) %collective-permute-start.4) | collective-permute-done | bytes 196640 | tf_op jit(solution)/shard_map/ppermute | solution.py:558
  27.8 3.1 %solve.1 = (f32[3,2,2,9]{3,2,1,0:T(2,128)}, f32[3,2,2,9]{3,2,1,0:T(2,128)}) custom-call(f32[384,128]{1,0:T(8,128)S(1)} %bitcast.11, f32[384,128]{1,0:T(8,128)S(1)} %bitcast.13), custom_call_target="tpu_custom_call" | custom-call | tf_op jit(solution)/shard_map/solve/pallas_call | solution.py:560
Async XLA Ops:
  2.5 4.5 %collective-permute-start.2 = (bf16[36,8,128]{2,1,0:T(8,128)(2,1)S(1)}, bf16[36,8,128]{2,1,0:T(8,128)(2,1)S(1)}, u32[]{:S(2)}, u32[]{:S(2)}) collective-permute-start(bf16[36,8,128]{2,1,0:T(8,128)(2,1)S(1)} %get-tuple-element.15), channel_id=1, source_target_pairs={{0,1},{1,0},{2,3},{3,2},{4,5},{5,4},{6,7},{7,6},{8,9},{9,8},{10,11... | collective-permute-start | bytes 221192 | tf_op jit(solution)/shard_map/ppermute | solution.py:499
  3.1 5.0 %collective-permute-start.3 = (bf16[36,8,128]{2,1,0:T(8,128)(2,1)S(1)}, bf16[36,8,128]{2,1,0:T(8,128)(2,1)S(1)}, u32[]{:S(2)}, u32[]{:S(2)}) collective-permute-start(bf16[36,8,128]{2,1,0:T(8,128)(2,1)S(1)} %get-tuple-element.16), channel_id=1, source_target_pairs={{0,8},{1,2},{2,1},{3,4},{4,3},{5,6},{6,5},{7,15},{8,0},{9,10},{10,... | collective-permute-start | bytes 221192 | tf_op jit(solution)/shard_map/ppermute | solution.py:499
  5.7 4.0 %collective-permute-start = (bf16[4,8,128]{2,1,0:T(8,128)(2,1)S(1)}, bf16[4,8,128]{2,1,0:T(8,128)(2,1)S(1)}, u32[]{:S(2)}, u32[]{:S(2)}) collective-permute-start(bf16[4,8,128]{2,1,0:T(8,128)(2,1)S(1)} %get-tuple-element.12), channel_id=1, source_target_pairs={{0,8},{1,9},{2,10},{3,11},{4,12},{5,13},{6,14},{7,15},{8,0},{9,1},... | collective-permute-start | bytes 24584 | tf_op jit(solution)/shard_map/ppermute | solution.py:499
  5.8 3.9 %collective-permute-start.1 = (bf16[4,8,128]{2,1,0:T(8,128)(2,1)S(1)}, bf16[4,8,128]{2,1,0:T(8,128)(2,1)S(1)}, u32[]{:S(2)}, u32[]{:S(2)}) collective-permute-start(bf16[4,8,128]{2,1,0:T(8,128)(2,1)S(1)} %get-tuple-element.13), channel_id=1, source_target_pairs={{0,1},{1,0},{2,3},{3,2},{4,5},{5,4},{6,7},{7,6},{8,16},{9,17},{10,... | collective-permute-start | bytes 24584 | tf_op jit(solution)/shard_map/ppermute | solution.py:499
  8.0 1.7 %copy-start = (bf16[128,128]{1,0:T(8,128)(2,1)S(1)}, bf16[128,128]{1,0:T(8,128)(2,1)}, u32[]{:S(2)}) copy-start(bf16[128,128]{1,0:T(8,128)(2,1)} %constant.5.clone.z_ref) | copy-start | bytes 98308
  8.0 1.7 %copy-start.1 = (bf16[48,160]{1,0:T(8,128)(2,1)S(1)}, bf16[48,160]{1,0:T(8,128)(2,1)}, u32[]{:S(2)}) copy-start(bf16[48,160]{1,0:T(8,128)(2,1)} %constant.4.clone.w_ref) | copy-start | bytes 46084
  26.4 1.4 %collective-permute-start.4 = (f32[16,24,128]{2,1,0:T(8,128)S(1)}, f32[16,24,128]{2,1,0:T(8,128)S(1)}, u32[]{:S(2)}, u32[]{:S(2)}) collective-permute-start(f32[16,24,128]{2,1,0:T(8,128)S(1)} %all_to_all.5), channel_id=1, source_target_pairs={{0,1},{1,0},{2,3},{3,2},{4,5},{5,4},{6,7},{7,6},{8,9},{9,8},{10,11... | collective-permute-start | bytes 589832 | tf_op jit(solution)/shard_map/ppermute | solution.py:558

commit v6 on v5

--- a/solution.py
+++ b/solution.py
@@ -396,6 +396,7 @@
             return jnp.where(lane < 72, lanes(v, -36), lanes(v, 72))
         return jnp.where(lane < 36, lanes(v, -72), lanes(v, 36))
 
+    spread = {}
     for s in range(2):
         for tx in range(2):
             for ty in range(2):
@@ -408,8 +409,11 @@
                         spill = jnp.zeros(shape, f32)
                         for c in range(3):
                             for iy in range(2):
-                                moved = slots(rows[c * 8 + iy * 4 + s * 2 + ty], 12 + tz, c * 4 + iy)
-                                spill = jnp.where(slot == c * 4 + iy, moved, spill)
+                                key = (c, iy, s, ty)
+                                if key not in spread:
+                                    spread[key] = slots(rows[c * 8 + iy * 4 + s * 2 + ty], 12, c * 4 + iy)
+                                spill = jnp.where(slot == c * 4 + iy + tz, spread[key], spill)
+                        spill = slots(spill, tz, 0)
                         if ty == 0:
                             both = slots(rows[23], s * 2 + tz, 0)
                             spill = spill + from_below_y(jnp.where(corner, both, 0.0))

time: 31.1 us -> 31.1 us (level)
  no operation moved by 1% of the time
where the time goes in v6:
time: 31.1 us; the launch traced here: 30.9 us
  blocking collectives  15.9 us (51%)
  Pallas kernels  7.27 us (23%)
  starting transfers between devices  4.52 us (15%)
  waiting for transfers between devices  2.45 us (8%)
  between operations  0.69 us (2%)
    all_to_all x1, blocking collectives, local(): mine = lax.all_to_all(payload, ('gx', 'gy'), 0, 0, axis_index_groups=groups)  15.9 us
    ppermute x4, starting transfers between devices, exchange(): return lax.ppermute(value, ('gx', 'gy'), pairs)  4.52 us
    pallas_call x1, Pallas kernels, local(): pl.pallas_call(functools.partial(solve_kernel, gx, gy), out_shape=[out, o...  3.06 us
    pallas_call x1, Pallas kernels, local(): pl.pallas_call(functools.partial(pack_kernel, gy), out_shape=[packed, pac...  1.86 us
    pallas_call x1, Pallas kernels, local(): pl.pallas_call(functools.partial(interior_kernel, gy), out_shape=[jax.Sha...  1.66 us
    ppermute x1, waiting for transfers between devices, local(): other = lax.ppermute(mine, 'gy', [(i, i ^ 1) for i in range(gy)])  1.44 us
    ppermute x4, waiting for transfers between devices, exchange(): return lax.ppermute(value, ('gx', 'gy'), pairs)  1.01 us
    pallas_call x1, Pallas kernels, local(): pl.pallas_call(functools.partial(finish_kernel, gx), out_shape=jax.ShapeD...  0.69 us
  transfers between devices with their start and end apart: 5, of which 2 were waited for; matrix products, arithmetic and copies ran while one was open for 0% of the time, Pallas kernels for 5%

profile of v6, /device:TPU:0, one launch (start us, length us, event | category | flops | bytes accessed | tf_op | source)
XLA Modules:
  0.0 30.9 jit_solution(8362431516267079269)
XLA Ops:
  0.6 1.9 %pack.1 = (bf16[36,8,128]{2,1,0:T(8,128)(2,1)S(1)}, bf16[36,8,128]{2,1,0:T(8,128)(2,1)S(1)}, bf16[4,8,128]{2,1,0:T(8,128)(2,1)S(1)}, bf16[4,8,128]{2,1,0:T(8,128...) custom-call(bf16[32,4,8,128]{3,2,1,0:T(8,128)(2,1)} %bitcast.16, ...), custom_call_target="tpu_custom_call" | custom-call | tf_op jit(solution)/shard_map/pack/pallas_call | solution.py:516
  2.5 0.6 %collective-permute-start.2 = (bf16[36,8,128]{2,1,0:T(8,128)(2,1)S(1)}, bf16[36,8,128]{2,1,0:T(8,128)(2,1)S(1)}, u32[]{:S(2)}, u32[]{:S(2)}) collective-permute-start(bf16[36,8,128]{2,1,0:T(8,128)(2,1)S(1)} %get-tuple-element.15), channel_id=1, source_target_pairs={{0,1},{1,0},{2,3},{3,2},{4,5},{5,4},{6,7},{7,6},{8,9},{9,8},{10,11... | collective-permute-start | bytes 221192 | tf_op jit(solution)/shard_map/ppermute | solution.py:503
  3.1 2.6 %collective-permute-start.3 = (bf16[36,8,128]{2,1,0:T(8,128)(2,1)S(1)}, bf16[36,8,128]{2,1,0:T(8,128)(2,1)S(1)}, u32[]{:S(2)}, u32[]{:S(2)}) collective-permute-start(bf16[36,8,128]{2,1,0:T(8,128)(2,1)S(1)} %get-tuple-element.16), channel_id=1, source_target_pairs={{0,8},{1,2},{2,1},{3,4},{4,3},{5,6},{6,5},{7,15},{8,0},{9,10},{10,... | collective-permute-start | bytes 221192 | tf_op jit(solution)/shard_map/ppermute | solution.py:503
  5.7 0.1 collective-permute-start
  5.8 1.2 %collective-permute-start.1 = (bf16[4,8,128]{2,1,0:T(8,128)(2,1)S(1)}, bf16[4,8,128]{2,1,0:T(8,128)(2,1)S(1)}, u32[]{:S(2)}, u32[]{:S(2)}) collective-permute-start(bf16[4,8,128]{2,1,0:T(8,128)(2,1)S(1)} %get-tuple-element.13), channel_id=1, source_target_pairs={{0,1},{1,0},{2,3},{3,2},{4,5},{5,4},{6,7},{7,6},{8,16},{9,17},{10,... | collective-permute-start | bytes 24584 | tf_op jit(solution)/shard_map/ppermute | solution.py:503
  7.0 0.0 collective-permute-done.2.ra_ref
  7.0 1.0 %collective-permute-done.3.rb_ref = bf16[36,8,128]{2,1,0:T(8,128)(2,1)S(1)} collective-permute-done((bf16[36,8,128]{2,1,0:T(8,128)(2,1)S(1)}, bf16[36,8,128]{2,1,0:T(8,128)(2,1)S(1)}, u32[]{:S(2)}, u32[]{:S(2)}) %collective-permute-start.3) | collective-permute-done | bytes 73760 | tf_op jit(solution)/shard_map/ppermute | solution.py:503
  8.0 0.0 copy-start
  8.0 0.0 copy-start.1
  8.0 1.7 %interior.1 = (f32[160,1152]{1,0:T(8,128)S(1)}, f32[4,32,128]{2,1,0:T(8,128)S(1)}) custom-call(bf16[32,32,128]{2,1,0:T(8,128)(2,1)S(1)} %bitcast.9, bf16[32,32,128]{2,1,0:T(8,128)(2,1)S(1)} %bitcast.12, bf16[36,8,128]{2,1,0:T(8,128)(2,1)S(1)} %collective-permute-done.2.ra_ref, bf16[36,8,128]{2,1,0:T(8,128)(2,1)S(1)} %collective-permute-done.3.rb_ref, ...), custom_call_target="tpu_custom_call" | custom-call | flops 8000000 | bytes 2000000 | tf_op jit(solution)/shard_map/interior/pallas_call | solution.py:535
  9.7 0.0 collective-permute-done
  9.7 0.0 collective-permute-done.1
  9.7 0.0 copy-done
  9.7 0.0 copy-done.1
  9.7 0.7 %finish.1 = f32[16,24,128]{2,1,0:T(8,128)S(1)} custom-call(bf16[32,32,128]{2,1,0:T(8,128)(2,1)S(1)} %bitcast.10, bf16[32,128]{1,0:T(8,128)(2,1)S(1)} %bitcast.14, bf16[32,128]{1,0:T(8,128)(2,1)S(1)} %bitcast.15, f32[4,32,128]{2,1,0:T(8,128)S(1)} %get-tuple-element.18.edge, f32[160,1152]{1,0:T(8,128)S(1)} %get-tuple-element.19.moment, ...), custom_call_target="tpu_custom_call" | custom-call | tf_op jit(solution)/shard_map/finish/pallas_call | solution.py:552
  10.4 15.9 %all_to_all.5 = f32[16,24,128]{2,1,0:T(8,128)S(1)} all-to-all(f32[16,24,128]{2,1,0:T(8,128)S(1)} %finish.1), channel_id=1, replica_groups={{0,2,4,6,8,10,12,14,16,18,20,22,24,26,28,30},{1,3,5,7,9,11,13,15,17,19,..., dimensions={0} | all-to-all | bytes 393216 | tf_op jit(solution)/shard_map/all_to_all | solution.py:561
  26.4 0.0 collective-permute-start.4
  26.4 1.4 %collective-permute-done.4 = f32[16,24,128]{2,1,0:T(8,128)S(1)} collective-permute-done((f32[16,24,128]{2,1,0:T(8,128)S(1)}, f32[16,24,128]{2,1,0:T(8,128)S(1)}, u32[]{:S(2)}, u32[]{:S(2)}) %collective-permute-start.4) | collective-permute-done | bytes 196640 | tf_op jit(solution)/shard_map/ppermute | solution.py:562
  27.8 3.1 %solve.1 = (f32[3,2,2,9]{3,2,1,0:T(2,128)}, f32[3,2,2,9]{3,2,1,0:T(2,128)}) custom-call(f32[384,128]{1,0:T(8,128)S(1)} %bitcast.11, f32[384,128]{1,0:T(8,128)S(1)} %bitcast.13), custom_call_target="tpu_custom_call" | custom-call | tf_op jit(solution)/shard_map/solve/pallas_call | solution.py:564
Async XLA Ops:
  2.5 4.5 %collective-permute-start.2 = (bf16[36,8,128]{2,1,0:T(8,128)(2,1)S(1)}, bf16[36,8,128]{2,1,0:T(8,128)(2,1)S(1)}, u32[]{:S(2)}, u32[]{:S(2)}) collective-permute-start(bf16[36,8,128]{2,1,0:T(8,128)(2,1)S(1)} %get-tuple-element.15), channel_id=1, source_target_pairs={{0,1},{1,0},{2,3},{3,2},{4,5},{5,4},{6,7},{7,6},{8,9},{9,8},{10,11... | collective-permute-start | bytes 221192 | tf_op jit(solution)/shard_map/ppermute | solution.py:503
  3.1 5.0 %collective-permute-start.3 = (bf16[36,8,128]{2,1,0:T(8,128)(2,1)S(1)}, bf16[36,8,128]{2,1,0:T(8,128)(2,1)S(1)}, u32[]{:S(2)}, u32[]{:S(2)}) collective-permute-start(bf16[36,8,128]{2,1,0:T(8,128)(2,1)S(1)} %get-tuple-element.16), channel_id=1, source_target_pairs={{0,8},{1,2},{2,1},{3,4},{4,3},{5,6},{6,5},{7,15},{8,0},{9,10},{10,... | collective-permute-start | bytes 221192 | tf_op jit(solution)/shard_map/ppermute | solution.py:503
  5.7 4.0 %collective-permute-start = (bf16[4,8,128]{2,1,0:T(8,128)(2,1)S(1)}, bf16[4,8,128]{2,1,0:T(8,128)(2,1)S(1)}, u32[]{:S(2)}, u32[]{:S(2)}) collective-permute-start(bf16[4,8,128]{2,1,0:T(8,128)(2,1)S(1)} %get-tuple-element.12), channel_id=1, source_target_pairs={{0,8},{1,9},{2,10},{3,11},{4,12},{5,13},{6,14},{7,15},{8,0},{9,1},... | collective-permute-start | bytes 24584 | tf_op jit(solution)/shard_map/ppermute | solution.py:503
  5.8 3.9 %collective-permute-start.1 = (bf16[4,8,128]{2,1,0:T(8,128)(2,1)S(1)}, bf16[4,8,128]{2,1,0:T(8,128)(2,1)S(1)}, u32[]{:S(2)}, u32[]{:S(2)}) collective-permute-start(bf16[4,8,128]{2,1,0:T(8,128)(2,1)S(1)} %get-tuple-element.13), channel_id=1, source_target_pairs={{0,1},{1,0},{2,3},{3,2},{4,5},{5,4},{6,7},{7,6},{8,16},{9,17},{10,... | collective-permute-start | bytes 24584 | tf_op jit(solution)/shard_map/ppermute | solution.py:503
  8.0 1.7 %copy-start = (bf16[128,128]{1,0:T(8,128)(2,1)S(1)}, bf16[128,128]{1,0:T(8,128)(2,1)}, u32[]{:S(2)}) copy-start(bf16[128,128]{1,0:T(8,128)(2,1)} %constant.5.clone.z_ref) | copy-start | bytes 98308
  8.0 1.7 %copy-start.1 = (bf16[48,160]{1,0:T(8,128)(2,1)S(1)}, bf16[48,160]{1,0:T(8,128)(2,1)}, u32[]{:S(2)}) copy-start(bf16[48,160]{1,0:T(8,128)(2,1)} %constant.4.clone.w_ref) | copy-start | bytes 46084
  26.4 1.4 %collective-permute-start.4 = (f32[16,24,128]{2,1,0:T(8,128)S(1)}, f32[16,24,128]{2,1,0:T(8,128)S(1)}, u32[]{:S(2)}, u32[]{:S(2)}) collective-permute-start(f32[16,24,128]{2,1,0:T(8,128)S(1)} %all_to_all.5), channel_id=1, source_target_pairs={{0,1},{1,0},{2,3},{3,2},{4,5},{5,4},{6,7},{7,6},{8,9},{9,8},{10,11... | collective-permute-start | bytes 589832 | tf_op jit(solution)/shard_map/ppermute | solution.py:562
